TPU v7x, 32 devices: a whole 2x2x4 slice. The times are simulated.
32 devices in a mesh: win: 2 (over x), sub: 16 (over z, y, core).
Axes of the slice: x: 2, y: 2, z: 4, core: 2. Of those that a mesh axis runs over, the one named last changes fastest.
Arguments:
- pulses: bfloat16 [32, 80, 2, 4096], P(('win', 'sub')), parts along dimension 0, may hold values from -6 to 6
- offsets: int32 [32, 80], P(('win', 'sub')), parts along dimension 0, may hold values from 0 to 3968
- geometry: float32 [32, 3, 80], P(('win', 'sub')), parts along dimension 0, may hold values from -1 to 1
- counts: int32 [32], P(('win', 'sub')), parts along dimension 0, may hold values from 48 to 80, as said below
Outputs:
- frames: float32 [32, 2, 32, 512], P(('win', 'sub')), parts along dimension 0
- cumulative: float32 [32, 2, 32, 512], P(('win', 'sub')), parts along dimension 0
There are 2 independent parts, one for each index of `win`. A program takes and returns all parts, laid end to end along the dimension named above; each array names one. Nothing has to cross between parts.
Inputs may be any that keep to these rules, and one draw needn't show every extreme that they name: Subaperture s holds its pulses in slots 0 to counts[s] - 1; the other slots are unused. Some subaperture has 80 pulses and some 48.
All inputs are finite; a program needn't handle non-finite values.
Results may differ from a plain program's by a relative error of at most 0.004.
Values sent between devices are 32-bit elements; how exact they have to be, the bound alone decides.
A program may use at most 192 MiB of HBM per device.

v0:
```python
import math

import jax
import jax.numpy as jnp
from jax import lax
from jax.sharding import PartitionSpec as P

ROWS = 32
COLS = 512
BINS = 128


def spectrum_of(pulse_rows, vertical_offset_along, geometry_sub, count, width):
    slots = pulse_rows.shape[0]
    windows = jax.vmap(lambda one_row, offset: lax.dynamic_slice_in_dim(one_row, offset, width, 1))(
        pulse_rows, vertical_offset_along
    ).astype(jnp.float32)
    index = jnp.arange(width, dtype=jnp.int32)
    shifted = index - width // 2
    turns = index[:, None] * shifted[None, :] % width
    angle = 2.0 * math.pi / width * turns.astype(jnp.float32)
    cosine = jnp.cos(angle)
    sine = jnp.sin(angle)
    highest = lax.Precision.HIGHEST
    real_in = windows[:, 0]
    imag_in = windows[:, 1]
    real_out = (
        jnp.dot(real_in, cosine, precision=highest) + jnp.dot(imag_in, sine, precision=highest)
    ) / width
    imag_out = (
        jnp.dot(imag_in, cosine, precision=highest) - jnp.dot(real_in, sine, precision=highest)
    ) / width
    viewing_bearing = 2.0 * math.pi * (shifted.astype(jnp.float32) / width + 0.37)
    scene_middle = width / 2.0 + width / 16.0 * geometry_sub[0]
    radar_frequency = 2.0 * math.pi / 100.0 * (37 * vertical_offset_along % 100).astype(jnp.float32)
    signal_argument = viewing_bearing[None, :] * scene_middle[:, None] + radar_frequency[:, None]
    live = (jnp.arange(slots, dtype=jnp.int32) < count).astype(jnp.float32) / math.sqrt(slots)
    cos_phase = jnp.cos(signal_argument)
    sin_phase = jnp.sin(signal_argument)
    coefficient_real = live[:, None] * (real_out * cos_phase - imag_out * sin_phase)
    coef_im = live[:, None] * (real_out * sin_phase + imag_out * cos_phase)
    return (coefficient_real, coef_im, viewing_bearing)


def block_product(
    coefficient_real, coef_im, viewing_bearing, row_slope, column_gradient, rows, cols
):
    xpos = (jnp.arange(rows, dtype=jnp.int32) - rows // 2).astype(jnp.float32)
    ypos = (jnp.arange(cols, dtype=jnp.int32) - cols // 2).astype(jnp.float32)
    angle_x = xpos[:, None, None] * (viewing_bearing[None, :] * row_slope[:, None])[None]
    cosine_x = jnp.cos(angle_x)
    sine_x = jnp.sin(angle_x)
    left_re = coefficient_real[None] * cosine_x - coef_im[None] * sine_x
    left_im = coefficient_real[None] * sine_x + coef_im[None] * cosine_x
    left = jnp.concatenate([left_re.reshape(rows, -1), left_im.reshape(rows, -1)], axis=1).astype(
        jnp.bfloat16
    )
    angle_y = (viewing_bearing[None, :] * column_gradient[:, None])[:, :, None] * ypos[
        None, None, :
    ]
    right_re = jnp.cos(angle_y).reshape(-1, cols)
    right_im = jnp.sin(angle_y).reshape(-1, cols)
    upper = jnp.concatenate([right_re, right_im], axis=1)
    lower = jnp.concatenate([-right_im, right_re], axis=1)
    right = jnp.concatenate([upper, lower], axis=0).astype(jnp.bfloat16)
    return jnp.dot(left, right, preferred_element_type=jnp.float32)


def shards(pulses, offsets, geometry, counts):
    rows = ROWS
    cols = COLS
    width = BINS
    slots = pulses.shape[1]
    count = counts[0]
    geometry_sub = geometry[0]
    coefficient_real, coef_im, viewing_bearing = spectrum_of(
        pulses[0], offsets[0], geometry_sub, count, width
    )
    row_slope = 0.05 * geometry_sub[1]
    column_gradient = 0.05 * geometry_sub[2]

    def add_block(step, total):
        start = (step * 8).astype(jnp.int32)
        part_re = lax.dynamic_slice_in_dim(coefficient_real, start, 8, 0)
        part_im = lax.dynamic_slice_in_dim(coef_im, start, 8, 0)
        slope_r = lax.dynamic_slice_in_dim(row_slope, start, 8, 0)
        slope_c = lax.dynamic_slice_in_dim(column_gradient, start, 8, 0)
        return total + block_product(
            part_re, part_im, viewing_bearing, slope_r, slope_c, rows, cols
        )

    empty = jnp.zeros((rows, 2 * cols), jnp.float32)
    total = lax.fori_loop(0, slots // 8, add_block, empty)
    own = jnp.stack([total[:, :cols], total[:, cols:]], axis=0)[None]
    flattened = own.reshape(1, 2 * rows * cols)
    by_pixels = lax.all_to_all(flattened, "sub", split_axis=1, concat_axis=0, tiled=True)
    members = by_pixels.shape[0]
    running = jnp.cumsum(by_pixels, axis=0)
    delayed = jnp.concatenate([jnp.zeros((8, running.shape[1]), jnp.float32), running[:-8]], axis=0)
    frame_rows = (running - delayed) / math.sqrt(8.0)
    magnitude_factor = jnp.sqrt(jnp.arange(1, members + 1, dtype=jnp.int32).astype(jnp.float32))
    cumulative_rows = running / magnitude_factor[:, None]
    frames_back, cumulative_back = (
        lax.all_to_all(frame_rows, "sub", split_axis=0, concat_axis=1, tiled=True),
        lax.all_to_all(cumulative_rows, "sub", split_axis=0, concat_axis=1, tiled=True),
    )
    frames = frames_back.reshape(1, 2, rows, cols)
    cumulative = cumulative_back.reshape(1, 2, rows, cols)
    return (frames, cumulative)


def solution(mesh):
    return jax.shard_map(
        shards,
        mesh=mesh,
        in_specs=(
            P(("win", "sub"), None, None, None),
            P(("win", "sub"), None),
            P(("win", "sub"), None, None),
            P(("win", "sub")),
        ),
        out_specs=(P(("win", "sub"), None, None, None), P(("win", "sub"), None, None, None)),
        check_vma=False,
    )
```

profile of v0, /device:TPU:0, one launch (start us, length us, event | category | flops | bytes accessed | tf_op | source)
XLA Modules:
  0.0 226.4 jit_solution(11494692594200224226)
XLA Ops:
  0.7 56.8 %copy.10 = bf16[1,80,2,4096]{2,1,3,0:T(8,128)(2,1)} copy(bf16[1,80,2,4096]{3,2,1,0:T(2,128)(2,1)} %param.6) | data formatting | bytes 2621440 | tf_op args[0]
  57.5 17.9 %gather_fusion = bf16[80,2,128]{1,0,2:T(8,128)(2,1)S(1)} fusion(bf16[80,2,4096]{1,0,2:T(8,128)(2,1)} %bitcast.1, s32[80]{0:T(128)S(1)} %fusion.56), kind=kCustom, calls=%fused_computation | custom fusion | bytes 82880 | tf_op jit(solution)/shard_map/vmap()/gather | solution.py:15
  75.3 3.2 %fusion.73 = (bf16[80,1,128]{1,0,2:T(8,128)(2,1)}, bf16[80,1,128]{1,0,2:T(8,128)(2,1)}) fusion(bf16[80,2,128]{1,0,2:T(8,128)(2,1)S(1)} %gather_fusion), kind=kLoop, calls=%fused_computation.101 | loop fusion | bytes 81920 | tf_op jit(solution)/shard_map/slice | solution.py:25
  78.5 3.1 %copy.11 = bf16[80,1,128]{2,0,1:T(8,128)(2,1)S(1)} copy(bf16[80,1,128]{1,0,2:T(8,128)(2,1)} %get-tuple-element.243) | data formatting | bytes 40960 | tf_op jit(solution)/shard_map/slice | solution.py:25
  81.6 1.6 copy.12
  83.2 0.4 fusion.43
  83.6 0.4 fusion.41
  84.1 0.4 fusion.30
  85.2 0.4 add_multiply_fusion.1
  85.6 100.0 %while.17 = (s32[]{:T(128)}, f32[32,1024]{1,0:T(8,128)S(1)}, f32[80,128]{1,0:T(8,128)S(1)}, f32[80]{0:T(128)S(1)}, f32[80,128]{1,0:T(8,128)S(1)}, /*index=5*/f32...) while((s32[]{:T(128)}, f32[32,1024]{1,0:T(8,128)S(1)}, ...), condition=%wide.region_1.2_spmd.clone.clone, body=%wide.region_0.1_spmd.clone.clone.sunk | while | flops 154242752 | bytes 6879337 | solution.py:93
  85.9 0.1 dynamic_slice.55
  86.0 0.6 fusion.82
  86.8 8.2 %fusion.81 = (bf16[1024,512]{1,0:T(8,128)(2,1)S(1)}, bf16[1024,512]{1,0:T(8,128)(2,1)S(1)}, bf16[1024,512]{1,0:T(8,128)(2,1)S(1)}) fusion(f32[512]{0:T(512)S(1)} %add_convert_fusion.4, f32[1024]{0:T(1024)S(1)} %bitcast_multiply_fusion.4), kind=kLoop, calls=%fused_computation.13.clone.1 | loop fusion | flops 2621440 | bytes 3151872 | tf_op jit(solution)/shard_map/convert.5
  95.0 0.8 fusion.83
  96.0 0.6 fusion.82
  96.6 0.1 dynamic_slice.54
  96.7 8.2 %fusion.81 = (bf16[1024,512]{1,0:T(8,128)(2,1)S(1)}, bf16[1024,512]{1,0:T(8,128)(2,1)S(1)}, bf16[1024,512]{1,0:T(8,128)(2,1)S(1)}) fusion(f32[512]{0:T(512)S(1)} %add_convert_fusion.4, f32[1024]{0:T(1024)S(1)} %bitcast_multiply_fusion.4), kind=kLoop, calls=%fused_computation.13.clone.1 | loop fusion | flops 2621440 | bytes 3151872 | tf_op jit(solution)/shard_map/convert.5
  105.0 0.8 fusion.83
  106.0 0.6 fusion.82
  106.6 0.1 dynamic_slice.54
  106.7 8.2 %fusion.81 = (bf16[1024,512]{1,0:T(8,128)(2,1)S(1)}, bf16[1024,512]{1,0:T(8,128)(2,1)S(1)}, bf16[1024,512]{1,0:T(8,128)(2,1)S(1)}) fusion(f32[512]{0:T(512)S(1)} %add_convert_fusion.4, f32[1024]{0:T(1024)S(1)} %bitcast_multiply_fusion.4), kind=kLoop, calls=%fused_computation.13.clone.1 | loop fusion | flops 2621440 | bytes 3151872 | tf_op jit(solution)/shard_map/convert.5
  114.9 0.8 fusion.83
  115.8 0.1 dynamic_slice.55
  116.0 0.6 fusion.82
  116.7 8.2 %fusion.81 = (bf16[1024,512]{1,0:T(8,128)(2,1)S(1)}, bf16[1024,512]{1,0:T(8,128)(2,1)S(1)}, bf16[1024,512]{1,0:T(8,128)(2,1)S(1)}) fusion(f32[512]{0:T(512)S(1)} %add_convert_fusion.4, f32[1024]{0:T(1024)S(1)} %bitcast_multiply_fusion.4), kind=kLoop, calls=%fused_computation.13.clone.1 | loop fusion | flops 2621440 | bytes 3151872 | tf_op jit(solution)/shard_map/convert.5
  124.9 0.8 fusion.83
  125.8 0.1 dynamic_slice.55
  126.0 0.6 fusion.82
  126.7 8.2 %fusion.81 = (bf16[1024,512]{1,0:T(8,128)(2,1)S(1)}, bf16[1024,512]{1,0:T(8,128)(2,1)S(1)}, bf16[1024,512]{1,0:T(8,128)(2,1)S(1)}) fusion(f32[512]{0:T(512)S(1)} %add_convert_fusion.4, f32[1024]{0:T(1024)S(1)} %bitcast_multiply_fusion.4), kind=kLoop, calls=%fused_computation.13.clone.1 | loop fusion | flops 2621440 | bytes 3151872 | tf_op jit(solution)/shard_map/convert.5
  134.9 0.8 fusion.83
  135.9 0.6 fusion.82
  136.7 8.2 %fusion.81 = (bf16[1024,512]{1,0:T(8,128)(2,1)S(1)}, bf16[1024,512]{1,0:T(8,128)(2,1)S(1)}, bf16[1024,512]{1,0:T(8,128)(2,1)S(1)}) fusion(f32[512]{0:T(512)S(1)} %add_convert_fusion.4, f32[1024]{0:T(1024)S(1)} %bitcast_multiply_fusion.4), kind=kLoop, calls=%fused_computation.13.clone.1 | loop fusion | flops 2621440 | bytes 3151872 | tf_op jit(solution)/shard_map/convert.5
  144.9 0.8 fusion.83
  145.7 0.1 dynamic_slice.55
  145.9 0.6 fusion.82
  146.5 0.1 dynamic_slice.54
  146.6 8.2 %fusion.81 = (bf16[1024,512]{1,0:T(8,128)(2,1)S(1)}, bf16[1024,512]{1,0:T(8,128)(2,1)S(1)}, bf16[1024,512]{1,0:T(8,128)(2,1)S(1)}) fusion(f32[512]{0:T(512)S(1)} %add_convert_fusion.4, f32[1024]{0:T(1024)S(1)} %bitcast_multiply_fusion.4), kind=kLoop, calls=%fused_computation.13.clone.1 | loop fusion | flops 2621440 | bytes 3151872 | tf_op jit(solution)/shard_map/convert.5
  154.9 0.8 fusion.83
  155.9 0.6 fusion.82
  156.6 8.2 %fusion.81 = (bf16[1024,512]{1,0:T(8,128)(2,1)S(1)}, bf16[1024,512]{1,0:T(8,128)(2,1)S(1)}, bf16[1024,512]{1,0:T(8,128)(2,1)S(1)}) fusion(f32[512]{0:T(512)S(1)} %add_convert_fusion.4, f32[1024]{0:T(1024)S(1)} %bitcast_multiply_fusion.4), kind=kLoop, calls=%fused_computation.13.clone.1 | loop fusion | flops 2621440 | bytes 3151872 | tf_op jit(solution)/shard_map/convert.5
  164.8 0.8 fusion.83
  165.9 0.6 fusion.82
  166.4 0.1 dynamic_slice.54
  166.6 8.2 %fusion.81 = (bf16[1024,512]{1,0:T(8,128)(2,1)S(1)}, bf16[1024,512]{1,0:T(8,128)(2,1)S(1)}, bf16[1024,512]{1,0:T(8,128)(2,1)S(1)}) fusion(f32[512]{0:T(512)S(1)} %add_convert_fusion.4, f32[1024]{0:T(1024)S(1)} %bitcast_multiply_fusion.4), kind=kLoop, calls=%fused_computation.13.clone.1 | loop fusion | flops 2621440 | bytes 3151872 | tf_op jit(solution)/shard_map/convert.5
  174.8 0.8 fusion.83
  175.7 0.1 dynamic_slice.55
  175.8 0.6 fusion.82
  176.6 8.2 %fusion.81 = (bf16[1024,512]{1,0:T(8,128)(2,1)S(1)}, bf16[1024,512]{1,0:T(8,128)(2,1)S(1)}, bf16[1024,512]{1,0:T(8,128)(2,1)S(1)}) fusion(f32[512]{0:T(512)S(1)} %add_convert_fusion.4, f32[1024]{0:T(1024)S(1)} %bitcast_multiply_fusion.4), kind=kLoop, calls=%fused_computation.13.clone.1 | loop fusion | flops 2621440 | bytes 3151872 | tf_op jit(solution)/shard_map/convert.5
  184.8 0.8 fusion.83
  185.7 0.8 all_to_all.30
  186.5 7.2 %all-to-all-start = ((f32[1,16,2048]{2,0,1:T(1,128)}), f32[1,16,2048]{2,0,1:T(1,128)S(1)}, u32[]{:S(2)}, u32[]{:S(2)}) async-start(f32[1,16,2048]{2,0,1:T(1,128)} %all_to_all.30), calls=%async_computation | async-start | bytes 262144 | tf_op jit(solution)/shard_map/all_to_all | solution.py:96
  193.7 7.9 %all-to-all-done = f32[1,16,2048]{2,0,1:T(1,128)S(1)} async-done(((f32[1,16,2048]{2,0,1:T(1,128)}), f32[1,16,2048]{2,0,1:T(1,128)S(1)}, u32[]{:S(2)}, u32[]{:S(2)}) %all-to-all-start) | async-done | bytes 131104 | tf_op jit(solution)/shard_map/all_to_all | solution.py:96
  201.7 0.1 reduce_window_sum.13
  201.8 0.8 copy.13
  202.6 3.5 %all-to-all-start.1 = ((f32[16,1,2048]{2,1,0:T(1,128)}), f32[16,1,2048]{2,1,0:T(1,128)S(1)}, u32[]{:S(2)}, u32[]{:S(2)}) async-start(f32[16,1,2048]{2,1,0:T(1,128)} %copy.13), calls=%async_computation.1 | async-start | bytes 262144 | tf_op jit(solution)/shard_map/all_to_all | solution.py:104
  206.1 0.1 bitcast_divide_fusion
  206.2 0.8 copy.14
  207.0 7.0 %all-to-all-done.1 = f32[16,1,2048]{2,1,0:T(1,128)S(1)} async-done(((f32[16,1,2048]{2,1,0:T(1,128)}), f32[16,1,2048]{2,1,0:T(1,128)S(1)}, u32[]{:S(2)}, u32[]{:S(2)}) %all-to-all-start.1) | async-done | bytes 131104 | tf_op jit(solution)/shard_map/all_to_all | solution.py:104
  214.0 3.5 %all-to-all-start.2 = ((f32[16,1,2048]{2,1,0:T(1,128)}), f32[16,1,2048]{2,1,0:T(1,128)S(1)}, u32[]{:S(2)}, u32[]{:S(2)}) async-start(f32[16,1,2048]{2,1,0:T(1,128)} %copy.14), calls=%async_computation.2 | async-start | bytes 262144 | tf_op jit(solution)/shard_map/all_to_all | solution.py:105
  217.5 0.3 reduce
  217.8 0.7 reshape.260
  218.5 6.9 %all-to-all-done.2 = f32[16,1,2048]{2,1,0:T(1,128)S(1)} async-done(((f32[16,1,2048]{2,1,0:T(1,128)}), f32[16,1,2048]{2,1,0:T(1,128)S(1)}, u32[]{:S(2)}, u32[]{:S(2)}) %all-to-all-start.2) | async-done | bytes 131104 | tf_op jit(solution)/shard_map/all_to_all | solution.py:105
  225.4 0.3 reduce.1
  225.7 0.7 reshape.261
  (109 shorter events, 2.8 us)
Async XLA Ops:
  0.7 56.8 %copy-start.2 = (s32[1,80]{1,0:T(1,128)S(1)}, s32[1,80]{1,0:T(1,128)}, u32[]{:S(2)}) copy-start(s32[1,80]{1,0:T(1,128)} %param.7) | copy-start | bytes 964
  78.5 3.1 %copy-start = (bf16[80,1,128]{1,0,2:T(8,128)(2,1)S(1)}, bf16[80,1,128]{1,0,2:T(8,128)(2,1)}, u32[]{:S(2)}) copy-start(bf16[80,1,128]{1,0,2:T(8,128)(2,1)} %get-tuple-element.244) | copy-start | bytes 61444
  78.5 6.0 %copy-start.1 = (f32[1,3,80]{2,0,1:T(1,128)S(1)}, f32[1,3,80]{2,0,1:T(1,128)}, u32[]{:S(2)}) copy-start(f32[1,3,80]{2,0,1:T(1,128)} %param.8) | copy-start | bytes 2884
  186.5 15.1 %all-to-all-start = ((f32[1,16,2048]{2,0,1:T(1,128)}), f32[1,16,2048]{2,0,1:T(1,128)S(1)}, u32[]{:S(2)}, u32[]{:S(2)}) async-start(f32[1,16,2048]{2,0,1:T(1,128)} %all_to_all.30), calls=%async_computation | async-start | bytes 262144 | tf_op jit(solution)/shard_map/all_to_all | solution.py:96
  202.6 11.4 %all-to-all-start.1 = ((f32[16,1,2048]{2,1,0:T(1,128)}), f32[16,1,2048]{2,1,0:T(1,128)S(1)}, u32[]{:S(2)}, u32[]{:S(2)}) async-start(f32[16,1,2048]{2,1,0:T(1,128)} %copy.13), calls=%async_computation.1 | async-start | bytes 262144 | tf_op jit(solution)/shard_map/all_to_all | solution.py:104
  214.0 11.4 %all-to-all-start.2 = ((f32[16,1,2048]{2,1,0:T(1,128)}), f32[16,1,2048]{2,1,0:T(1,128)S(1)}, u32[]{:S(2)}, u32[]{:S(2)}) async-start(f32[16,1,2048]{2,1,0:T(1,128)} %copy.14), calls=%async_computation.2 | async-start | bytes 262144 | tf_op jit(solution)/shard_map/all_to_all | solution.py:105
where the time goes:
time: 228 us; the launch traced here: 226 us
  other arithmetic  89.6 us (39%)
  local copies, waits for them, and re-layouts  88.8 us (39%)
  waiting for transfers between devices  21.8 us (10%)
  starting transfers between devices  14.3 us (6%)
  matrix products  9.7 us (4%)
    another operation x20, other arithmetic  87.8 us
    unnamed x8, local copies, waits for them, and re-layouts  56.8 us
    gather x1, local copies, waits for them, and re-layouts, spectrum_of(): lax.dynamic_slice_in_dim(one_row, offset, width, 1)  17.9 us
    dot_general x10, matrix products, block_product(): return jnp.dot(left, right, preferred_element_type=jnp.float32)  7.96 us
    all_to_all x1, waiting for transfers between devices, shards(): lax.all_to_all(flattened, 'sub', split_axis=1, concat_axis=0, tiled=True)  7.89 us
    all_to_all x1, starting transfers between devices, shards(): lax.all_to_all(flattened, 'sub', split_axis=1, concat_axis=0, tiled=True)  7.24 us
    all_to_all x1, waiting for transfers between devices, shards(): lax.all_to_all(frame_rows, 'sub', split_axis=0, concat_axis=1, tiled=True)  7 us
    all_to_all x1, waiting for transfers between devices, shards(): lax.all_to_all(cumulative_rows, 'sub', split_axis=0, concat_axis=1, tiled...  6.86 us
  transfers between devices with their start and end apart: 3, of which 3 were waited for; matrix products, arithmetic and copies ran while one was open for 1% of the time, Pallas kernels for 0%

commit v1 on v0

v1 whole, which is shorter than its diff:
```python
import functools
import math

import jax
import jax.numpy as jnp
import numpy as np
from jax import lax
from jax.experimental import pallas as pl
from jax.experimental.pallas import tpu as pltpu
from jax.sharding import PartitionSpec as P

ROWS = 32
COLS = 512
BINS = 128
GROUP = 4
HIGHEST = lax.Precision.HIGHEST

_N = 4001


def _sine_series():
    u = 0.25 * np.cos(np.pi * (np.arange(_N) + 0.5) / _N)
    basis = np.stack([u ** (2 * k + 1) for k in range(6)], axis=1)
    scale = np.abs(basis).max(axis=0)
    fit = np.linalg.lstsq(basis / scale, np.sin(2.0 * np.pi * u), rcond=None)[0] / scale
    return [float(np.float32(c)) for c in fit]


SINE = _sine_series()


def quarter_sine(u):
    z = u * u
    total = SINE[5]
    for k in (4, 3, 2, 1, 0):
        total = total * z + SINE[k]
    return total * u


def cos_sin(turns):
    r = turns - jnp.round(turns)
    a = jnp.abs(r)
    s = quarter_sine(jnp.minimum(a, 0.5 - a))
    return quarter_sine(0.25 - a), jnp.where(r < 0, -s, s)


def frequency_order(width):
    order = []
    for j in range(width // 16):
        order += [16 * j + 8 + l for l in range(8)] + [16 * j + 7 - l for l in range(8)]
    return np.array(order)


def tables(width, rows, cols):
    order = frequency_order(width)
    g = order - width // 2
    b = np.arange(width)
    angle = 2.0 * np.pi * ((b[:, None] * g[None, :]) % width) / width
    dft = np.concatenate([np.cos(angle), np.sin(angle)], axis=1) / width
    tau = g / width + 0.37
    m = np.arange(1, cols // 2 + 1)
    l = np.arange(8)
    middles = (16 * np.arange(width // 16) + 7.5 - width // 2) / width + 0.37
    side = ((l + 0.5) / width)[:, None] * m[None, :] * 0.05
    middle = middles[:, None] * m[None, :] * 0.05
    row = l[:, None] * tau[None, :] * 0.05
    lead = np.stack([tau, g], axis=0)
    f32 = np.float32
    return (
        dft.astype(f32),
        np.concatenate([side, middle], axis=0).astype(f32),
        row.astype(f32),
        lead.astype(f32),
    )


def own_image(
    offs_s, geo_s, count_s, pulses, offs_v, geo_v, dft, column, row, lead, win, coef, acc, rows, cols
):
    slots, width = pulses.shape[1], dft.shape[0]
    half = cols // 2
    last = pulses.shape[3] // width - 2
    lanes = lax.broadcasted_iota(jnp.int32, (2, width), 1)

    def fetch(p):
        offset = offs_s[0, p]
        block = jnp.minimum(offset // width, last)
        rest = offset - block * width
        first = pulses[0, p, :, pl.ds(pl.multiple_of(block * width, width), width)]
        second = pulses[0, p, :, pl.ds(pl.multiple_of(block * width + width, width), width)]
        both = jnp.where(
            lanes >= rest, first.astype(jnp.float32), second.astype(jnp.float32)
        )
        win[pl.ds(p, 1), :] = both[0:1]
        win[pl.ds(slots + p, 1), :] = both[1:2]

    def fetch_some(i, _):
        for k in range(8):
            fetch(i * 8 + k)
        return 0

    lax.fori_loop(0, slots // 8, fetch_some, 0)

    out = jnp.dot(win[...], dft[...], precision=HIGHEST, preferred_element_type=jnp.float32)
    spec_re = out[:slots, :width] + out[slots:, width:]
    spec_im = out[slots:, :width] - out[:slots, width:]

    eye = lax.broadcasted_iota(jnp.int32, (slots, slots), 0) == lax.broadcasted_iota(
        jnp.int32, (slots, slots), 1
    )

    def upright(line):
        return jnp.sum(jnp.where(eye, line, 0.0), axis=1, keepdims=True)

    offset_line = offs_v[...]
    block_line = jnp.minimum(offset_line // width, last)
    rest = upright((offset_line - block_line * width).astype(jnp.float32))
    carrier = upright((37 * offset_line % 100).astype(jnp.float32) / 100.0)
    centre = width / 2.0 + width / 16.0 * upright(geo_v[0, 0:1, :])
    slope = 0.05 * upright(geo_v[0, 1:2, :])
    tau = lead[0:1, :]
    turned = lead[1:2, :] * rest * (1.0 / width)
    phase = tau * centre
    phase = (phase - jnp.round(phase)) + carrier + (turned - jnp.round(turned))
    live = jnp.where(
        lax.broadcasted_iota(jnp.int32, (slots, 1), 0) < count_s[0], 1.0 / math.sqrt(slots), 0.0
    )
    spec_re = spec_re * live
    spec_im = spec_im * live
    blocks = rows // 8
    for q in range(blocks):
        c, s = cos_sin(phase + tau * slope * float(8 * q - rows // 2))
        coef[2 * q] = spec_re * c - spec_im * s
        coef[2 * q + 1] = spec_re * s + spec_im * c

    acc[...] = jnp.zeros_like(acc)

    def pulse(p):
        cx, sx = cos_sin(row[...] * geo_s[0, 1, p])
        real, imag = [], []
        for q in range(blocks):
            cr = coef[2 * q, pl.ds(p, 1), :]
            ci = coef[2 * q + 1, pl.ds(p, 1), :]
            real.append(cr * cx - ci * sx)
            imag.append(cr * sx + ci * cx)
        left = jnp.concatenate(real + imag, axis=0).astype(jnp.bfloat16)
        cy, sy = cos_sin(column[...] * geo_s[0, 2, p])
        c0, s0 = cy[:8], sy[:8]
        right_c, right_s = [], []
        for j in range(width // 16):
            cm, sm = cy[8 + j : 9 + j], sy[8 + j : 9 + j]
            cc, ss, sc, cs = cm * c0, sm * s0, sm * c0, cm * s0
            right_c += [cc - ss, cc + ss]
            right_s += [sc + cs, sc - cs]
        right = jnp.concatenate(
            [
                jnp.concatenate(right_c, axis=0).astype(jnp.bfloat16),
                jnp.concatenate(right_s, axis=0).astype(jnp.bfloat16),
            ],
            axis=1,
        )
        return left, right

    def step(i, total):
        lefts, rights = [], []
        for k in range(GROUP):
            left, right = pulse(i * GROUP + k)
            total = total + left.astype(jnp.float32)
            lefts.append(left)
            rights.append(right)
        acc[...] += jnp.dot(
            jnp.concatenate(lefts, axis=1),
            jnp.concatenate(rights, axis=0),
            preferred_element_type=jnp.float32,
        )
        return total

    total = lax.fori_loop(
        0, slots // GROUP, step, jnp.zeros((2 * rows, width), jnp.float32)
    )
    zero = jnp.sum(total, axis=1, keepdims=True)
    rc, rs = acc[:rows, :half], acc[:rows, half:]
    ic, is_ = acc[rows:, :half], acc[rows:, half:]
    ahead = jnp.concatenate([rc - is_, rs + ic], axis=0)
    behind = jnp.concatenate([rc + is_, ic - rs], axis=0)
    flip = (
        lax.broadcasted_iota(jnp.int32, (half, half), 0)
        + lax.broadcasted_iota(jnp.int32, (half, half), 1)
        == half - 1
    ).astype(jnp.float32)
    low = jnp.dot(behind, flip, precision=HIGHEST, preferred_element_type=jnp.float32)
    high = pltpu.roll(ahead, 1, 1)
    high = jnp.where(lax.broadcasted_iota(jnp.int32, high.shape, 1) == 0, zero, high)
    return low, high


def image_kernel(
    offs_s, geo_s, count_s, pulses, offs_v, geo_v, dft, column, row, lead, image, win, coef, acc
):
    low, high = own_image(
        offs_s, geo_s, count_s, pulses, offs_v, geo_v, dft, column, row, lead, win, coef, acc, ROWS, COLS
    )
    image[:, : COLS // 2] = low
    image[:, COLS // 2 :] = high


def shards(pulses, offsets, geometry, counts):
    rows, cols, width = ROWS, COLS, BINS
    slots = pulses.shape[1]
    constants = [jnp.asarray(t) for t in tables(width, rows, cols)]
    smem = pl.BlockSpec(memory_space=pltpu.SMEM)
    vmem = pl.BlockSpec(memory_space=pltpu.VMEM)
    total = pl.pallas_call(
        image_kernel,
        out_shape=jax.ShapeDtypeStruct((2 * rows, cols), jnp.float32),
        in_specs=[smem] * 3 + [vmem] * 7,
        out_specs=vmem,
        scratch_shapes=[
            pltpu.VMEM((2 * slots, width), jnp.float32),
            pltpu.VMEM((2 * (rows // 8), slots, width), jnp.float32),
            pltpu.VMEM((2 * rows, cols), jnp.float32),
        ],
    )(offsets, geometry, counts, pulses, offsets, geometry, *constants)
    flattened = total.reshape(1, 2 * rows * cols)
    by_pixels = lax.all_to_all(flattened, "sub", split_axis=1, concat_axis=0, tiled=True)
    members = by_pixels.shape[0]
    running = jnp.cumsum(by_pixels, axis=0)
    delayed = jnp.concatenate([jnp.zeros((8, running.shape[1]), jnp.float32), running[:-8]], axis=0)
    frame_rows = (running - delayed) / math.sqrt(8.0)
    magnitude_factor = jnp.sqrt(jnp.arange(1, members + 1, dtype=jnp.int32).astype(jnp.float32))
    cumulative_rows = running / magnitude_factor[:, None]
    frames_back, cumulative_back = (
        lax.all_to_all(frame_rows, "sub", split_axis=0, concat_axis=1, tiled=True),
        lax.all_to_all(cumulative_rows, "sub", split_axis=0, concat_axis=1, tiled=True),
    )
    return (
        frames_back.reshape(1, 2, rows, cols),
        cumulative_back.reshape(1, 2, rows, cols),
    )


def solution(mesh):
    return jax.shard_map(
        shards,
        mesh=mesh,
        in_specs=(
            P(("win", "sub"), None, None, None),
            P(("win", "sub"), None),
            P(("win", "sub"), None, None),
            P(("win", "sub")),
        ),
        out_specs=(P(("win", "sub"), None, None, None), P(("win", "sub"), None, None, None)),
        check_vma=False,
    )
```

time: 228 us -> 55.6 us (0.24)
  other arithmetic: 89.6 us -> 0.85 us
  local copies, waits for them, and re-layouts: 88.8 us -> 5.96 us
  Pallas kernels: 0 us -> 10.7 us
  matrix products: 9.7 us -> 0 us
    another operation x21 -> x0, other arithmetic: 87.8 us -> none
    unnamed x8 -> x2, local copies, waits for them, and re-layouts: 56.8 us -> 1.3 us
    gather x1 -> x0, local copies, waits for them, and re-layouts: 17.9 us -> none  [spectrum_of(): lax.dynamic_slice_in_dim(one_row, offset, width, 1)]
    pallas_call x0 -> x1, Pallas kernels: none -> 10.7 us  [shards(): pl.pallas_call(image_kernel, out_shape=jax.ShapeDtypeStruct((2 * rows, co...]
    dot_general x14 -> x0, matrix products: 9.7 us -> none  [the longest x10 7.96 us: block_product(): return jnp.dot(left, right, preferred_element_type=jnp.float32)]
    slice x3 -> x0, local copies, waits for them, and re-layouts: 7.82 us -> none  [the longest x2 6.27 us: spectrum_of(): real_in = windows[:, 0]]
  transfers between devices with their start and end apart: 3 -> 3, of which waited for: 3 -> 3; matrix products, arithmetic and copies ran while one was open for 1% -> 3% of each run, Pallas kernels for 0% -> 0%
where the time goes in v1:
time: 55.6 us; the launch traced here: 55.1 us
  waiting for transfers between devices  21.8 us (39%)
  starting transfers between devices  14.4 us (26%)
  Pallas kernels  10.7 us (19%)
  local copies, waits for them, and re-layouts  5.96 us (11%)
  between operations  1.35 us (2%)
  other arithmetic  0.85 us (2%)
    pallas_call x1, Pallas kernels, shards(): pl.pallas_call(image_kernel, out_shape=jax.ShapeDtypeStruct((2 * rows, co...  10.7 us
    all_to_all x1, waiting for transfers between devices, shards(): lax.all_to_all(flattened, 'sub', split_axis=1, concat_axis=0, tiled=True)  7.89 us
    all_to_all x1, starting transfers between devices, shards(): lax.all_to_all(flattened, 'sub', split_axis=1, concat_axis=0, tiled=True)  7.41 us
    all_to_all x1, waiting for transfers between devices, shards(): lax.all_to_all(frame_rows, 'sub', split_axis=0, concat_axis=1, tiled=True)  7.01 us
    all_to_all x1, waiting for transfers between devices, shards(): lax.all_to_all(cumulative_rows, 'sub', split_axis=0, concat_axis=1, tiled...  6.86 us
    all_to_all x1, starting transfers between devices, shards(): lax.all_to_all(frame_rows, 'sub', split_axis=0, concat_axis=1, tiled=True)  3.51 us
    all_to_all x1, starting transfers between devices, shards(): lax.all_to_all(cumulative_rows, 'sub', split_axis=0, concat_axis=1, tiled...  3.51 us
    all_to_all x1, local copies, waits for them, and re-layouts, shards(): lax.all_to_all(flattened, 'sub', split_axis=1, concat_axis=0, tiled=True)  1.71 us
  transfers between devices with their start and end apart: 3, of which 3 were waited for; matrix products, arithmetic and copies ran while one was open for 3% of the time, Pallas kernels for 0%

profile of v1, /device:TPU:0, one launch (start us, length us, event | category | flops | bytes accessed | tf_op | source)
XLA Modules:
  0.0 55.1 jit_solution(13947431427222352088)
XLA Ops:
  1.3 1.3 %copy.12.geo_s.geo_v = f32[1,3,80]{2,1,0:T(4,128)} copy(f32[1,3,80]{2,0,1:T(1,128)} %param.10) | data formatting | bytes 1920 | tf_op args[2]
  2.5 10.7 %shard_map.95 = f32[64,512]{1,0:T(8,128)} custom-call(s32[1,80]{1,0:T(1,128)} %offs_v.1, f32[1,3,80]{2,1,0:T(4,128)} %copy.12.geo_s.geo_v, s32[1]{0:T(128)S(6)} %copy.20.count_s, bf16[1,80,2,4096]{3,2,1,0:T(2,128)(2,1)} %pulses.1, s32[1,80]{1,0:T(1,128)} %offs_v.1, f32[1,3,80]{2,1,0:T(4,128)} %copy.12.geo_s.geo_v, f32[128,256]{1,0:T(8,128)} %constant.18.clone.dft, ...), custom_call_target="tpu_custom_call" | custom-call | tf_op jit(solution)/shard_map/pallas_call | solution.py:213
  13.3 1.7 %all_to_all.36 = f32[1,16,2048]{2,0,1:T(1,128)} reshape(f32[64,512]{1,0:T(8,128)} %shard_map.95) | data formatting | bytes 262144 | tf_op jit(solution)/shard_map/all_to_all | solution.py:225
  15.0 7.4 %all-to-all-start = ((f32[1,16,2048]{2,0,1:T(1,128)}), f32[1,16,2048]{2,0,1:T(1,128)S(1)}, u32[]{:S(2)}, u32[]{:S(2)}) async-start(f32[1,16,2048]{2,0,1:T(1,128)} %all_to_all.36), calls=%async_computation | async-start | bytes 262144 | tf_op jit(solution)/shard_map/all_to_all | solution.py:225
  22.4 7.9 %all-to-all-done = f32[1,16,2048]{2,0,1:T(1,128)S(1)} async-done(((f32[1,16,2048]{2,0,1:T(1,128)}), f32[1,16,2048]{2,0,1:T(1,128)S(1)}, u32[]{:S(2)}, u32[]{:S(2)}) %all-to-all-start) | async-done | bytes 131104 | tf_op jit(solution)/shard_map/all_to_all | solution.py:225
  30.3 0.1 reduce_window_sum.13
  30.5 0.8 %copy.15 = f32[16,1,2048]{2,1,0:T(1,128)} copy(f32[16,1,2048]{2,0,1:T(8,128)S(1)} %multiply_bitcast_fusion) | data formatting | bytes 262144 | tf_op jit(solution)/shard_map/all_to_all | solution.py:233
  31.3 3.5 %all-to-all-start.1 = ((f32[16,1,2048]{2,1,0:T(1,128)}), f32[16,1,2048]{2,1,0:T(1,128)S(1)}, u32[]{:S(2)}, u32[]{:S(2)}) async-start(f32[16,1,2048]{2,1,0:T(1,128)} %copy.15), calls=%async_computation.1 | async-start | bytes 262144 | tf_op jit(solution)/shard_map/all_to_all | solution.py:233
  34.8 0.1 bitcast_divide_fusion
  34.9 0.8 %copy.16 = f32[16,1,2048]{2,1,0:T(1,128)} copy(f32[16,1,2048]{2,0,1:T(8,128)S(1)} %bitcast_divide_fusion) | data formatting | bytes 262144 | tf_op jit(solution)/shard_map/div | solution.py:231
  35.7 7.0 %all-to-all-done.1 = f32[16,1,2048]{2,1,0:T(1,128)S(1)} async-done(((f32[16,1,2048]{2,1,0:T(1,128)}), f32[16,1,2048]{2,1,0:T(1,128)S(1)}, u32[]{:S(2)}, u32[]{:S(2)}) %all-to-all-start.1) | async-done | bytes 131104 | tf_op jit(solution)/shard_map/all_to_all | solution.py:233
  42.7 3.5 %all-to-all-start.2 = ((f32[16,1,2048]{2,1,0:T(1,128)}), f32[16,1,2048]{2,1,0:T(1,128)S(1)}, u32[]{:S(2)}, u32[]{:S(2)}) async-start(f32[16,1,2048]{2,1,0:T(1,128)} %copy.16), calls=%async_computation.2 | async-start | bytes 262144 | tf_op jit(solution)/shard_map/all_to_all | solution.py:234
  46.2 0.3 reduce
  46.5 0.7 %reshape.63 = f32[1,2,32,512]{3,2,1,0:T(8,128)} reshape(f32[16,2048]{1,0:T(8,128)S(1)} %reduce) | data formatting | bytes 262144 | tf_op jit(solution)/shard_map/reshape | solution.py:237
  47.2 6.9 %all-to-all-done.2 = f32[16,1,2048]{2,1,0:T(1,128)S(1)} async-done(((f32[16,1,2048]{2,1,0:T(1,128)}), f32[16,1,2048]{2,1,0:T(1,128)S(1)}, u32[]{:S(2)}, u32[]{:S(2)}) %all-to-all-start.2) | async-done | bytes 131104 | tf_op jit(solution)/shard_map/all_to_all | solution.py:234
  54.1 0.3 reduce.1
  54.4 0.7 %reshape.64 = f32[1,2,32,512]{3,2,1,0:T(8,128)} reshape(f32[16,2048]{1,0:T(8,128)S(1)} %reduce.1) | data formatting | bytes 262144 | tf_op jit(solution)/shard_map/reshape | solution.py:238
  (4 shorter events, 0.1 us)
Async XLA Ops:
  15.0 15.3 %all-to-all-start = ((f32[1,16,2048]{2,0,1:T(1,128)}), f32[1,16,2048]{2,0,1:T(1,128)S(1)}, u32[]{:S(2)}, u32[]{:S(2)}) async-start(f32[1,16,2048]{2,0,1:T(1,128)} %all_to_all.36), calls=%async_computation | async-start | bytes 262144 | tf_op jit(solution)/shard_map/all_to_all | solution.py:225
  31.3 11.4 %all-to-all-start.1 = ((f32[16,1,2048]{2,1,0:T(1,128)}), f32[16,1,2048]{2,1,0:T(1,128)S(1)}, u32[]{:S(2)}, u32[]{:S(2)}) async-start(f32[16,1,2048]{2,1,0:T(1,128)} %copy.15), calls=%async_computation.1 | async-start | bytes 262144 | tf_op jit(solution)/shard_map/all_to_all | solution.py:233
  42.7 11.4 %all-to-all-start.2 = ((f32[16,1,2048]{2,1,0:T(1,128)}), f32[16,1,2048]{2,1,0:T(1,128)S(1)}, u32[]{:S(2)}, u32[]{:S(2)}) async-start(f32[16,1,2048]{2,1,0:T(1,128)} %copy.16), calls=%async_computation.2 | async-start | bytes 262144 | tf_op jit(solution)/shard_map/all_to_all | solution.py:234

commit v2 on v1

--- a/solution.py
+++ b/solution.py
@@ -74,11 +74,8 @@
     )
 
 
-def own_image(
-    offs_s, geo_s, count_s, pulses, offs_v, geo_v, dft, column, row, lead, win, coef, acc, rows, cols
-):
-    slots, width = pulses.shape[1], dft.shape[0]
-    half = cols // 2
+def fetch_kernel(offs_s, pulses, win):
+    slots, width = pulses.shape[1], win.shape[1]
     last = pulses.shape[3] // width - 2
     lanes = lax.broadcasted_iota(jnp.int32, (2, width), 1)
 
@@ -101,6 +98,11 @@
 
     lax.fori_loop(0, slots // 8, fetch_some, 0)
 
+
+def own_image(geo_s, count_s, win, offs_v, geo_v, dft, column, row, lead, coef, acc, last, rows, cols):
+    slots, width = offs_v.shape[1], dft.shape[0]
+    half = cols // 2
+
     out = jnp.dot(win[...], dft[...], precision=HIGHEST, preferred_element_type=jnp.float32)
     spec_re = out[:slots, :width] + out[slots:, width:]
     spec_im = out[slots:, :width] - out[:slots, width:]
@@ -116,8 +118,8 @@
     block_line = jnp.minimum(offset_line // width, last)
     rest = upright((offset_line - block_line * width).astype(jnp.float32))
     carrier = upright((37 * offset_line % 100).astype(jnp.float32) / 100.0)
-    centre = width / 2.0 + width / 16.0 * upright(geo_v[0, 0:1, :])
-    slope = 0.05 * upright(geo_v[0, 1:2, :])
+    centre = width / 2.0 + width / 16.0 * upright(geo_v[0])
+    slope = 0.05 * upright(geo_v[1])
     tau = lead[0:1, :]
     turned = lead[1:2, :] * rest * (1.0 / width)
     phase = tau * centre
@@ -136,7 +138,7 @@
     acc[...] = jnp.zeros_like(acc)
 
     def pulse(p):
-        cx, sx = cos_sin(row[...] * geo_s[0, 1, p])
+        cx, sx = cos_sin(row[...] * geo_s[1, 0, p])
         real, imag = [], []
         for q in range(blocks):
             cr = coef[2 * q, pl.ds(p, 1), :]
@@ -144,7 +146,7 @@
             real.append(cr * cx - ci * sx)
             imag.append(cr * sx + ci * cx)
         left = jnp.concatenate(real + imag, axis=0).astype(jnp.bfloat16)
-        cy, sy = cos_sin(column[...] * geo_s[0, 2, p])
+        cy, sy = cos_sin(column[...] * geo_s[2, 0, p])
         c0, s0 = cy[:8], sy[:8]
         right_c, right_s = [], []
         for j in range(width // 16):
@@ -194,49 +196,157 @@
     return low, high
 
 
-def image_kernel(
-    offs_s, geo_s, count_s, pulses, offs_v, geo_v, dft, column, row, lead, image, win, coef, acc
+def kernel(
+    members,
+    last,
+    geo_s,
+    count_s,
+    win,
+    offs_v,
+    geo_v,
+    dft,
+    column,
+    row,
+    lead,
+    frames,
+    cumulative,
+    coef,
+    acc,
+    mine,
+    shares,
+    sums,
+    back,
+    send_a,
+    recv_a,
+    send_b,
+    recv_b,
 ):
+    me = lax.axis_index("sub")
+    flat = members <= 32
+
+    def others(body):
+        def go(d, _):
+            body(lax.rem(me + d, members))
+            return 0
+
+        lax.fori_loop(1, members, go, 0, unroll=flat)
+
+    barrier = pltpu.get_barrier_semaphore()
+    others(lambda peer: pl.semaphore_signal(barrier, inc=1, device_id={"sub": peer}))
+
+    rows, cols = ROWS, COLS
+    half = cols // 2
     low, high = own_image(
-        offs_s, geo_s, count_s, pulses, offs_v, geo_v, dft, column, row, lead, win, coef, acc, ROWS, COLS
-    )
-    image[:, : COLS // 2] = low
-    image[:, COLS // 2 :] = high
+        geo_s, count_s, win, offs_v, geo_v, dft, column, row, lead, coef, acc, last, rows, cols
+    )
+    tall = 2 * rows
+    share = mine.shape[1]
+    each = tall // share
+    for c in range(cols // 128):
+        part = low if c * 128 < half else high
+        at = c * 128 % half
+        for k in range(each):
+            mine[c * each + k] = part[k * share : (k + 1) * share, at : at + 128]
+    shares[me] = mine[me]
+
+    pl.semaphore_wait(barrier, members - 1)
+
+    def first(peer):
+        return pltpu.make_async_remote_copy(
+            src_ref=mine.at[peer],
+            dst_ref=shares.at[me],
+            send_sem=send_a.at[peer],
+            recv_sem=recv_a.at[me],
+            device_id={"sub": peer},
+        )
+
+    def first_in(peer):
+        return pltpu.make_async_remote_copy(
+            src_ref=mine.at[peer],
+            dst_ref=shares.at[peer],
+            send_sem=send_a.at[peer],
+            recv_sem=recv_a.at[peer],
+            device_id={"sub": peer},
+        )
+
+    others(lambda peer: first(peer).start())
+    others(lambda peer: first_in(peer).wait_recv())
+
+    running = []
+    for s in range(members):
+        running.append(shares[s] if s == 0 else running[-1] + shares[s])
+        frame = running[s] if s < 8 else running[s] - running[s - 8]
+        sums[s, 0] = frame * (1.0 / math.sqrt(8.0))
+        sums[s, 1] = running[s] * (1.0 / math.sqrt(s + 1.0))
+    back[me] = sums[me]
+
+    def second(peer):
+        return pltpu.make_async_remote_copy(
+            src_ref=sums.at[peer],
+            dst_ref=back.at[me],
+            send_sem=send_b.at[peer],
+            recv_sem=recv_b.at[me],
+            device_id={"sub": peer},
+        )
+
+    def second_in(peer):
+        return pltpu.make_async_remote_copy(
+            src_ref=sums.at[peer],
+            dst_ref=back.at[peer],
+            send_sem=send_b.at[peer],
+            recv_sem=recv_b.at[peer],
+            device_id={"sub": peer},
+        )
+
+    others(lambda peer: second(peer).start())
+    others(lambda peer: first(peer).wait_send())
+    others(lambda peer: second_in(peer).wait_recv())
+    for j in range(members):
+        c, k = j // each, j % each
+        at = slice(k * share, (k + 1) * share), slice(c * 128, (c + 1) * 128)
+        frames[at] = back[j, 0]
+        cumulative[at] = back[j, 1]
+    others(lambda peer: second(peer).wait_send())
 
 
 def shards(pulses, offsets, geometry, counts):
     rows, cols, width = ROWS, COLS, BINS
     slots = pulses.shape[1]
+    members = lax.axis_size("sub")
     constants = [jnp.asarray(t) for t in tables(width, rows, cols)]
+    track = jnp.transpose(geometry, (1, 0, 2))
     smem = pl.BlockSpec(memory_space=pltpu.SMEM)
     vmem = pl.BlockSpec(memory_space=pltpu.VMEM)
-    total = pl.pallas_call(
-        image_kernel,
-        out_shape=jax.ShapeDtypeStruct((2 * rows, cols), jnp.float32),
-        in_specs=[smem] * 3 + [vmem] * 7,
+    share = 2 * rows * cols // 128 // members
+    whole = jax.ShapeDtypeStruct((2 * rows, cols), jnp.float32)
+    dma = pltpu.SemaphoreType.DMA((members,))
+    win = pl.pallas_call(
+        fetch_kernel,
+        out_shape=jax.ShapeDtypeStruct((2 * slots, width), jnp.float32),
+        in_specs=[smem, vmem],
         out_specs=vmem,
+    )(offsets, pulses)
+    last = pulses.shape[3] // width - 2
+    frames, cumulative = pl.pallas_call(
+        functools.partial(kernel, members, last),
+        out_shape=(whole, whole),
+        in_specs=[smem] * 2 + [vmem] * 7,
+        out_specs=(vmem, vmem),
         scratch_shapes=[
-            pltpu.VMEM((2 * slots, width), jnp.float32),
             pltpu.VMEM((2 * (rows // 8), slots, width), jnp.float32),
             pltpu.VMEM((2 * rows, cols), jnp.float32),
+            pltpu.VMEM((members, share, 128), jnp.float32),
+            pltpu.VMEM((members, share, 128), jnp.float32),
+            pltpu.VMEM((members, 2, share, 128), jnp.float32),
+            pltpu.VMEM((members, 2, share, 128), jnp.float32),
+            dma,
+            dma,
+            dma,
+            dma,
         ],
-    )(offsets, geometry, counts, pulses, offsets, geometry, *constants)
-    flattened = total.reshape(1, 2 * rows * cols)
-    by_pixels = lax.all_to_all(flattened, "sub", split_axis=1, concat_axis=0, tiled=True)
-    members = by_pixels.shape[0]
-    running = jnp.cumsum(by_pixels, axis=0)
-    delayed = jnp.concatenate([jnp.zeros((8, running.shape[1]), jnp.float32), running[:-8]], axis=0)
-    frame_rows = (running - delayed) / math.sqrt(8.0)
-    magnitude_factor = jnp.sqrt(jnp.arange(1, members + 1, dtype=jnp.int32).astype(jnp.float32))
-    cumulative_rows = running / magnitude_factor[:, None]
-    frames_back, cumulative_back = (
-        lax.all_to_all(frame_rows, "sub", split_axis=0, concat_axis=1, tiled=True),
-        lax.all_to_all(cumulative_rows, "sub", split_axis=0, concat_axis=1, tiled=True),
-    )
-    return (
-        frames_back.reshape(1, 2, rows, cols),
-        cumulative_back.reshape(1, 2, rows, cols),
-    )
+        compiler_params=pltpu.CompilerParams(collective_id=0, has_side_effects=True),
+    )(track, counts, win, offsets, track, *constants)
+    return frames.reshape(1, 2, rows, cols), cumulative.reshape(1, 2, rows, cols)
 
 
 def solution(mesh):

time: 55.6 us -> 31.6 us (0.57)
  waiting for transfers between devices: 21.8 us -> 0 us
  Pallas kernels: 10.7 us -> 27 us
  starting transfers between devices: 14.4 us -> 0 us
  local copies, waits for them, and re-layouts: 5.96 us -> 3.14 us
  other arithmetic: 0.85 us -> 0 us
    all_to_all x3 -> x0, waiting for transfers between devices: 21.8 us -> none  [the longest x1 7.89 us: shards(): lax.all_to_all(flattened, 'sub', split_axis=1, concat_axis=0, tiled=True)]
    pallas_call x1 -> x2, Pallas kernels: 10.7 us -> 27 us  [the longest x1 24.3 us: shards(): pl.pallas_call(functools.partial(kernel, members, last), out_shape=(whole...]
    all_to_all x3 -> x0, starting transfers between devices: 14.4 us -> none  [the longest x1 7.41 us: shards(): lax.all_to_all(flattened, 'sub', split_axis=1, concat_axis=0, tiled=True)]
    all_to_all x2 -> x0, local copies, waits for them, and re-layouts: 2.5 us -> none  [the longest x1 1.71 us: shards(): lax.all_to_all(flattened, 'sub', split_axis=1, concat_axis=0, tiled=True)]
    unnamed x2, local copies, waits for them, and re-layouts: 1.3 us -> 3.14 us
    reshape x2 -> x0, local copies, waits for them, and re-layouts: 1.39 us -> none  [the longest x1 0.69 us: shards(): frames_back.reshape(1, 2, rows, cols)]
    div x1 -> x0, local copies, waits for them, and re-layouts: 0.77 us -> none  [shards(): cumulative_rows = running / magnitude_factor[:, None]]
    all_to_all x3 -> x0, other arithmetic: 0.63 us -> none  [the longest x2 0.32 us: shards(): lax.all_to_all(frame_rows, 'sub', split_axis=0, concat_axis=1, tiled=True)]
  transfers between devices with their start and end apart: 3 -> 0, of which waited for: 3 -> 0; matrix products, arithmetic and copies ran while one was open for 3% -> 0% of each run, Pallas kernels for 0% -> 0%
where the time goes in v2:
time: 31.6 us; the launch traced here: 31.4 us
  Pallas kernels  27 us (85%)
  local copies, waits for them, and re-layouts  3.14 us (10%)
  between operations  1.29 us (4%)
    pallas_call x1, Pallas kernels, shards(): pl.pallas_call(functools.partial(kernel, members, last), out_shape=(whole...  24.3 us
    unnamed x2, local copies, waits for them, and re-layouts  3.14 us
    pallas_call x1, Pallas kernels, shards(): pl.pallas_call(fetch_kernel, out_shape=jax.ShapeDtypeStruct((2 * slots, w...  2.66 us

profile of v2, /device:TPU:0, one launch (start us, length us, event | category | flops | bytes accessed | tf_op | source)
XLA Modules:
  0.0 31.4 jit_solution(4343894869284349385)
XLA Ops:
  1.3 2.7 %shard_map.95.win = f32[160,128]{1,0:T(8,128)} custom-call(s32[1,80]{1,0:T(1,128)} %offs_v.1, bf16[1,80,2,4096]{3,2,1,0:T(2,128)(2,1)} %pulses.1), custom_call_target="tpu_custom_call" | custom-call | tf_op jit(solution)/shard_map/pallas_call | solution.py:323
  3.9 24.3 %shard_map.96 = (f32[64,512]{1,0:T(8,128)}, f32[64,512]{1,0:T(8,128)}) custom-call(f32[3,1,80]{2,1,0:T(1,128)} %bitcast.5, s32[1]{0:T(128)S(6)} %copy.12.count_s, f32[160,128]{1,0:T(8,128)} %shard_map.95.win, s32[1,80]{1,0:T(1,128)} %offs_v.1, f32[3,1,80]{2,1,0:T(1,128)} %bitcast.6, f32[128,256]{1,0:T(8,128)} %constant.8.clone.dft, ...), custom_call_target="tpu_custom_call" | custom-call | tf_op jit(solution)/shard_map/pallas_call | solution.py:330
  28.3 1.6 %copy.13 = f32[1,2,32,512]{3,2,1,0:T(8,128)} copy(f32[1,2,32,512]{3,2,1,0:T(8,128)} %bitcast.4) | data formatting | bytes 262144
  29.8 1.6 %copy.14 = f32[1,2,32,512]{3,2,1,0:T(8,128)} copy(f32[1,2,32,512]{3,2,1,0:T(8,128)} %bitcast.3) | data formatting | bytes 262144

commit v3 on v2

v3 whole, which is shorter than its diff:
```python
import functools
import math

import jax
import jax.numpy as jnp
import numpy as np
from jax import lax
from jax.experimental import pallas as pl
from jax.experimental.pallas import tpu as pltpu
from jax.sharding import PartitionSpec as P

ROWS = 32
COLS = 512
BINS = 128
GROUP = 4
HIGHEST = lax.Precision.HIGHEST

_N = 4001


def _sine_series():
    u = 0.25 * np.cos(np.pi * (np.arange(_N) + 0.5) / _N)
    basis = np.stack([u ** (2 * k + 1) for k in range(6)], axis=1)
    scale = np.abs(basis).max(axis=0)
    fit = np.linalg.lstsq(basis / scale, np.sin(2.0 * np.pi * u), rcond=None)[0] / scale
    return [float(np.float32(c)) for c in fit]


SINE = _sine_series()


def quarter_sine(u):
    z = u * u
    total = SINE[5]
    for k in (4, 3, 2, 1, 0):
        total = total * z + SINE[k]
    return total * u


def cos_sin(turns):
    r = turns - jnp.round(turns)
    a = jnp.abs(r)
    s = quarter_sine(jnp.minimum(a, 0.5 - a))
    return quarter_sine(0.25 - a), jnp.where(r < 0, -s, s)


def frequency_order(width):
    order = []
    for j in range(width // 16):
        order += [16 * j + 8 + l for l in range(8)] + [16 * j + 7 - l for l in range(8)]
    return np.array(order)


def tables(width, rows, cols):
    order = frequency_order(width)
    g = order - width // 2
    b = np.arange(width)
    angle = 2.0 * np.pi * ((b[:, None] * g[None, :]) % width) / width
    dft = np.concatenate([np.cos(angle), np.sin(angle)], axis=1) / width
    tau = g / width + 0.37
    m = np.arange(1, cols // 2 + 1)
    l = np.arange(8)
    middles = (16 * np.arange(width // 16) + 7.5 - width // 2) / width + 0.37
    side = ((l + 0.5) / width)[:, None] * m[None, :] * 0.05
    middle = middles[:, None] * m[None, :] * 0.05
    row = l[:, None] * tau[None, :] * 0.05
    lead = np.stack([tau, g], axis=0)
    f32 = np.float32
    return (
        dft.astype(f32),
        np.concatenate([side, middle], axis=0).astype(f32),
        row.astype(f32),
        lead.astype(f32),
    )


def fetch_kernel(offs_s, pulses, win):
    slots, width = pulses.shape[1], win.shape[1]
    last = pulses.shape[3] // width - 2
    lanes = lax.broadcasted_iota(jnp.int32, (2, width), 1)

    def fetch(p):
        offset = offs_s[0, p]
        block = jnp.minimum(offset // width, last)
        rest = offset - block * width
        first = pulses[0, p, :, pl.ds(pl.multiple_of(block * width, width), width)]
        second = pulses[0, p, :, pl.ds(pl.multiple_of(block * width + width, width), width)]
        both = jnp.where(
            lanes >= rest, first.astype(jnp.float32), second.astype(jnp.float32)
        )
        win[pl.ds(p, 1), :] = both[0:1]
        win[pl.ds(slots + p, 1), :] = both[1:2]

    def fetch_some(i, _):
        for k in range(8):
            fetch(i * 8 + k)
        return 0

    lax.fori_loop(0, slots // 8, fetch_some, 0)


def prepare(count_s, win, offs_v, geo_v, dft, lead, coef, last, rows):
    slots, width = offs_v.shape[1], dft.shape[0]

    out = jnp.dot(win[...], dft[...], precision=HIGHEST, preferred_element_type=jnp.float32)
    spec_re = out[:slots, :width] + out[slots:, width:]
    spec_im = out[slots:, :width] - out[:slots, width:]

    eye = lax.broadcasted_iota(jnp.int32, (slots, slots), 0) == lax.broadcasted_iota(
        jnp.int32, (slots, slots), 1
    )

    def upright(line):
        return jnp.sum(jnp.where(eye, line, 0.0), axis=1, keepdims=True)

    offset_line = offs_v[...]
    block_line = jnp.minimum(offset_line // width, last)
    rest = upright((offset_line - block_line * width).astype(jnp.float32))
    carrier = upright((37 * offset_line % 100).astype(jnp.float32) / 100.0)
    centre = width / 2.0 + width / 16.0 * upright(geo_v[0])
    slope = 0.05 * upright(geo_v[1])
    tau = lead[0:1, :]
    turned = lead[1:2, :] * rest * (1.0 / width)
    phase = tau * centre
    phase = (phase - jnp.round(phase)) + carrier + (turned - jnp.round(turned))
    live = jnp.where(
        lax.broadcasted_iota(jnp.int32, (slots, 1), 0) < count_s[0], 1.0 / math.sqrt(slots), 0.0
    )
    spec_re = spec_re * live
    spec_im = spec_im * live
    blocks = rows // 8
    for q in range(blocks):
        c, s = cos_sin(phase + tau * slope * float(8 * q - rows // 2))
        coef[2 * q] = spec_re * c - spec_im * s
        coef[2 * q + 1] = spec_re * s + spec_im * c


def lefts_of(p, geo_s, row, coef, rows):
    blocks = rows // 8
    cx, sx = cos_sin(row[...] * geo_s[1, 0, p])
    real, imag = [], []
    for q in range(blocks):
        cr = coef[2 * q, pl.ds(p, 1), :]
        ci = coef[2 * q + 1, pl.ds(p, 1), :]
        real.append(cr * cx - ci * sx)
        imag.append(cr * sx + ci * cx)
    return jnp.concatenate(real + imag, axis=0).astype(jnp.bfloat16)


def right_of(p, geo_s, column, at, width):
    cy, sy = cos_sin(column[:, at : at + 128] * geo_s[2, 0, p])
    c0, s0 = cy[:8], sy[:8]
    right_c, right_s = [], []
    for j in range(width // 16):
        cm, sm = cy[8 + j : 9 + j], sy[8 + j : 9 + j]
        cc, ss, sc, cs = cm * c0, sm * s0, sm * c0, cm * s0
        right_c += [cc - ss, cc + ss]
        right_s += [sc + cs, sc - cs]
    return jnp.concatenate(
        [
            jnp.concatenate(right_c, axis=0).astype(jnp.bfloat16),
            jnp.concatenate(right_s, axis=0).astype(jnp.bfloat16),
        ],
        axis=1,
    )


def one_pass(h, geo_s, column, row, coef, left_all, acc, slots, width, rows):
    acc[...] = jnp.zeros_like(acc)

    def step(i, total):
        rights = []
        for k in range(GROUP):
            p = i * GROUP + k
            if h == 0:
                left = lefts_of(p, geo_s, row, coef, rows)
                left_all[i, :, k * width : (k + 1) * width] = left
                total = total + left.astype(jnp.float32)
            rights.append(right_of(p, geo_s, column, 128 * h, width))
        acc[...] += jnp.dot(
            left_all[i],
            jnp.concatenate(rights, axis=0),
            preferred_element_type=jnp.float32,
        )
        return total

    if h == 0:
        total = lax.fori_loop(
            0, slots // GROUP, step, jnp.zeros((2 * rows, width), jnp.float32)
        )
        zero = jnp.sum(total, axis=1, keepdims=True)
    else:
        lax.fori_loop(0, slots // GROUP, step, 0)
        zero = None
    rc, rs = acc[:rows, :128], acc[:rows, 128:]
    ic, is_ = acc[rows:, :128], acc[rows:, 128:]
    ahead = jnp.concatenate([rc - is_, rs + ic], axis=0)
    behind = jnp.concatenate([rc + is_, ic - rs], axis=0)
    flip = (
        lax.broadcasted_iota(jnp.int32, (128, 128), 0)
        + lax.broadcasted_iota(jnp.int32, (128, 128), 1)
        == 127
    ).astype(jnp.float32)
    low = jnp.dot(behind, flip, precision=HIGHEST, preferred_element_type=jnp.float32)
    return low, ahead, zero


def kernel(
    members,
    last,
    geo_s,
    count_s,
    win,
    offs_v,
    geo_v,
    dft,
    column,
    row,
    lead,
    frames,
    cumulative,
    coef,
    left_all,
    acc,
    mine,
    shares,
    sums,
    back,
    send_a,
    recv_a,
    send_b,
    recv_b,
):
    me = lax.axis_index("sub")
    order = sorted(range(1, members), key=lambda d: abs(2 * d - members))

    def others(body):
        if members <= 32:
            for d in order:
                body(lax.rem(me + d, members))
            return

        def go(d, _):
            body(lax.rem(me + d, members))
            return 0

        lax.fori_loop(1, members, go, 0)

    barrier = pltpu.get_barrier_semaphore()
    others(lambda peer: pl.semaphore_signal(barrier, inc=1, device_id={"sub": peer}))

    rows, cols, width, slots = ROWS, COLS, BINS, offs_v.shape[1]
    passes = cols // 256
    tall = 2 * rows
    share = mine.shape[2]
    each = tall // share

    def copy_of(source, target, sends, recvs, h, peer, owner):
        return pltpu.make_async_remote_copy(
            src_ref=source.at[h, peer],
            dst_ref=target.at[h, owner],
            send_sem=sends.at[h, peer],
            recv_sem=recvs.at[h, owner],
            device_id={"sub": peer},
        )

    def first(h, peer, owner):
        return copy_of(mine, shares, send_a, recv_a, h, peer, owner)

    def second(h, peer, owner):
        return copy_of(sums, back, send_b, recv_b, h, peer, owner)

    prepare(count_s, win, offs_v, geo_v, dft, lead, coef, last, rows)
    before = None
    for h in range(passes):
        low, ahead, zero = one_pass(
            h, geo_s, column, row, coef, left_all, acc, slots, width, rows
        )
        high = pltpu.roll(ahead, 1, 1)
        edge = lax.broadcasted_iota(jnp.int32, high.shape, 1) == 0
        high = jnp.where(edge, zero if h == 0 else before, high)
        before = pltpu.roll(ahead, 1, 1)
        for k in range(each):
            mine[h, k] = low[k * share : (k + 1) * share]
            mine[h, each + k] = high[k * share : (k + 1) * share]
        shares[h, me] = mine[h, me]
        if h == 0:
            pl.semaphore_wait(barrier, members - 1)
        others(lambda peer: first(h, peer, me).start())

    for h in range(passes):
        others(lambda peer: first(h, peer, peer).wait_recv())
        running = []
        for s in range(members):
            running.append(shares[h, s] if s == 0 else running[-1] + shares[h, s])
            frame = running[s] if s < 8 else running[s] - running[s - 8]
            sums[h, s, 0] = frame * (1.0 / math.sqrt(8.0))
            sums[h, s, 1] = running[s] * (1.0 / math.sqrt(s + 1.0))
        back[h, me] = sums[h, me]
        others(lambda peer: second(h, peer, me).start())

    for h in range(passes):
        others(lambda peer: first(h, peer, me).wait_send())
    for h in range(passes):
        others(lambda peer: second(h, peer, peer).wait_recv())
        for j in range(members):
            k = j % each
            c = passes - 1 - h if j < each else passes + h
            at = slice(k * share, (k + 1) * share), slice(c * 128, (c + 1) * 128)
            frames[at] = back[h, j, 0]
            cumulative[at] = back[h, j, 1]
    for h in range(passes):
        others(lambda peer: second(h, peer, me).wait_send())


def shards(pulses, offsets, geometry, counts):
    rows, cols, width = ROWS, COLS, BINS
    slots = pulses.shape[1]
    members = lax.axis_size("sub")
    constants = [jnp.asarray(t) for t in tables(width, rows, cols)]
    track = jnp.transpose(geometry, (1, 0, 2))
    smem = pl.BlockSpec(memory_space=pltpu.SMEM)
    vmem = pl.BlockSpec(memory_space=pltpu.VMEM)
    passes = cols // 256
    share = 4 * rows // members
    whole = jax.ShapeDtypeStruct((2 * rows, cols), jnp.float32)
    dma = pltpu.SemaphoreType.DMA((passes, members))
    win = pl.pallas_call(
        fetch_kernel,
        out_shape=jax.ShapeDtypeStruct((2 * slots, width), jnp.float32),
        in_specs=[smem, vmem],
        out_specs=vmem,
        compiler_params=pltpu.CompilerParams(vmem_limit_bytes=16 * 2**20),
    )(offsets, pulses)
    last = pulses.shape[3] // width - 2
    frames, cumulative = pl.pallas_call(
        functools.partial(kernel, members, last),
        out_shape=(whole, whole),
        in_specs=[smem] * 2 + [vmem] * 7,
        out_specs=(vmem, vmem),
        scratch_shapes=[
            pltpu.VMEM((2 * (rows // 8), slots, width), jnp.float32),
            pltpu.VMEM((slots // GROUP, 2 * rows, GROUP * width), jnp.bfloat16),
            pltpu.VMEM((2 * rows, 256), jnp.float32),
            pltpu.VMEM((passes, members, share, 128), jnp.float32),
            pltpu.VMEM((passes, members, share, 128), jnp.float32),
            pltpu.VMEM((passes, members, 2, share, 128), jnp.float32),
            pltpu.VMEM((passes, members, 2, share, 128), jnp.float32),
            dma,
            dma,
            dma,
            dma,
        ],
        compiler_params=pltpu.CompilerParams(
            collective_id=0, has_side_effects=True, vmem_limit_bytes=16 * 2**20
        ),
    )(track, counts, win, offsets, track, *constants)
    return frames.reshape(1, 2, rows, cols), cumulative.reshape(1, 2, rows, cols)


def solution(mesh):
    return jax.shard_map(
        shards,
        mesh=mesh,
        in_specs=(
            P(("win", "sub"), None, None, None),
            P(("win", "sub"), None),
            P(("win", "sub"), None, None),
            P(("win", "sub")),
        ),
        out_specs=(P(("win", "sub"), None, None, None), P(("win", "sub"), None, None, None)),
        check_vma=False,
    )
```

time: 31.6 us -> 31.4 us (level)
  Pallas kernels: 27 us -> 26.5 us
    pallas_call x1, Pallas kernels: 2.66 us -> 1.24 us  [shards(): pl.pallas_call(fetch_kernel, out_shape=jax.ShapeDtypeStruct((2 * slots, w...]
    pallas_call x1, Pallas kernels: 24.3 us -> 25.3 us  [shards(): pl.pallas_call(functools.partial(kernel, members, last), out_shape=(whole...]
    unnamed x2 -> x16, local copies, waits for them, and re-layouts: 3.14 us -> 3.3 us
where the time goes in v3:
time: 31.4 us; the launch traced here: 31.2 us
  Pallas kernels  26.5 us (84%)
  local copies, waits for them, and re-layouts  3.3 us (11%)
  between operations  1.39 us (4%)
    pallas_call x1, Pallas kernels, shards(): pl.pallas_call(functools.partial(kernel, members, last), out_shape=(whole...  25.3 us
    unnamed x16, local copies, waits for them, and re-layouts  3.3 us
    pallas_call x1, Pallas kernels, shards(): pl.pallas_call(fetch_kernel, out_shape=jax.ShapeDtypeStruct((2 * slots, w...  1.24 us

profile of v3, /device:TPU:0, one launch (start us, length us, event | category | flops | bytes accessed | tf_op | source)
XLA Modules:
  0.0 31.2 jit_solution(10623532422108617222)
XLA Ops:
  0.6 0.0 copy-start.6
  0.6 0.0 copy-start.4
  0.7 0.0 copy-start.3
  1.3 0.0 copy-start
  1.3 1.3 %copy-done = bf16[1,80,2,4096]{3,2,1,0:T(2,128)(2,1)S(1)} copy-done((bf16[1,80,2,4096]{3,2,1,0:T(2,128)(2,1)S(1)}, bf16[1,80,2,4096]{3,2,1,0:T(2,128)(2,1)}, u32[]{:S(2)}) %copy-start) | copy-done | bytes 1310744
  2.7 0.0 copy-start.5
  2.7 0.7 %copy-done.5 = s32[1,80]{1,0:T(1,128)S(1)} copy-done((s32[1,80]{1,0:T(1,128)S(1)}, s32[1,80]{1,0:T(1,128)}, u32[]{:S(2)}) %copy-start.5) | copy-done | bytes 344
  3.3 0.0 copy-start.1
  3.3 0.0 copy-start.2
  3.3 1.2 %shard_map.95.win = f32[160,128]{1,0:T(8,128)S(1)} custom-call(s32[1,80]{1,0:T(1,128)S(1)} %copy-done.5, bf16[1,80,2,4096]{3,2,1,0:T(2,128)(2,1)S(1)} %copy-done), custom_call_target="tpu_custom_call" | custom-call | tf_op jit(solution)/shard_map/pallas_call | solution.py:328
  4.6 0.0 copy-done.6
  4.6 0.0 copy-done.4
  4.6 0.0 copy-done.3
  4.6 0.0 copy-done.1
  4.6 0.0 copy-done.2
  4.6 25.3 %shard_map.96 = (f32[64,512]{1,0:T(8,128)S(1)}, f32[64,512]{1,0:T(8,128)S(1)}) custom-call(f32[3,1,80]{2,1,0:T(1,128)S(1)} %bitcast.5, s32[1]{0:T(128)S(6)} %copy.12.count_s, f32[160,128]{1,0:T(8,128)S(1)} %shard_map.95.win, s32[1,80]{1,0:T(1,128)S(1)} %copy-done.5, f32[3,1,80]{2,1,0:T(1,128)S(1)} %bitcast.6, f32[128,256]{1,0:T(8,128)S(1)} %copy-done.1, ...), custom_call_target="tpu_custom_call" | custom-call | tf_op jit(solution)/shard_map/pallas_call | solution.py:336
  29.9 0.7 %copy.13 = f32[1,2,32,512]{3,2,1,0:T(8,128)} copy(f32[1,2,32,512]{3,2,1,0:T(8,128)S(1)} %bitcast.4) | data formatting | bytes 262144
  30.5 0.7 %copy.14 = f32[1,2,32,512]{3,2,1,0:T(8,128)} copy(f32[1,2,32,512]{3,2,1,0:T(8,128)S(1)} %bitcast.3) | data formatting | bytes 262144
Async XLA Ops:
  0.6 3.9 %copy-start.6 = (f32[2,128]{1,0:T(2,128)S(1)}, f32[2,128]{1,0:T(2,128)}, u32[]{:S(2)}) copy-start(f32[2,128]{1,0:T(2,128)} %constant.11.clone.lead) | copy-start | bytes 3076
  0.6 3.9 %copy-start.4 = (f32[8,128]{1,0:T(8,128)S(1)}, f32[8,128]{1,0:T(8,128)}, u32[]{:S(2)}) copy-start(f32[8,128]{1,0:T(8,128)} %constant.10.clone.row) | copy-start | bytes 12292
  0.7 3.9 %copy-start.3 = (f32[1,3,80]{2,0,1:T(1,128)S(1)}, f32[1,3,80]{2,0,1:T(1,128)}, u32[]{:S(2)}) copy-start(f32[1,3,80]{2,0,1:T(1,128)} %param.10) | copy-start | bytes 2884
  1.3 1.3 %copy-start = (bf16[1,80,2,4096]{3,2,1,0:T(2,128)(2,1)S(1)}, bf16[1,80,2,4096]{3,2,1,0:T(2,128)(2,1)}, u32[]{:S(2)}) copy-start(bf16[1,80,2,4096]{3,2,1,0:T(2,128)(2,1)} %pulses.1) | copy-start | bytes 3932164
  2.7 0.7 %copy-start.5 = (s32[1,80]{1,0:T(1,128)S(1)}, s32[1,80]{1,0:T(1,128)}, u32[]{:S(2)}) copy-start(s32[1,80]{1,0:T(1,128)} %offs_v.1) | copy-start | bytes 964
  3.3 1.3 %copy-start.1 = (f32[128,256]{1,0:T(8,128)S(1)}, f32[128,256]{1,0:T(8,128)}, u32[]{:S(2)}) copy-start(f32[128,256]{1,0:T(8,128)} %constant.8.clone.dft) | copy-start | bytes 393220
  3.3 1.3 %copy-start.2 = (f32[16,256]{1,0:T(8,128)S(1)}, f32[16,256]{1,0:T(8,128)}, u32[]{:S(2)}) copy-start(f32[16,256]{1,0:T(8,128)} %constant.9.clone.column) | copy-start | bytes 49156

commit v4 on v3

--- a/solution.py
+++ b/solution.py
@@ -12,36 +12,33 @@
 ROWS = 32
 COLS = 512
 BINS = 128
-GROUP = 4
+GROUP = 8
 HIGHEST = lax.Precision.HIGHEST
 
-_N = 4001
-
-
-def _sine_series():
-    u = 0.25 * np.cos(np.pi * (np.arange(_N) + 0.5) / _N)
-    basis = np.stack([u ** (2 * k + 1) for k in range(6)], axis=1)
+def _series(count, odd):
+    r = 0.5 * np.cos(np.pi * (np.arange(4001) + 0.5) / 4001)
+    basis = np.stack([r ** (2 * k + odd) for k in range(count)], axis=1)
     scale = np.abs(basis).max(axis=0)
-    fit = np.linalg.lstsq(basis / scale, np.sin(2.0 * np.pi * u), rcond=None)[0] / scale
+    wave = np.sin(2.0 * np.pi * r) if odd else np.cos(2.0 * np.pi * r)
+    fit = np.linalg.lstsq(basis / scale, wave, rcond=None)[0] / scale
     return [float(np.float32(c)) for c in fit]
 
 
-SINE = _sine_series()
-
-
-def quarter_sine(u):
-    z = u * u
-    total = SINE[5]
-    for k in (4, 3, 2, 1, 0):
-        total = total * z + SINE[k]
-    return total * u
+COSINE = _series(7, 0)
+SINE = _series(7, 1)
+
+
+def horner(z, series):
+    total = z * series[-1] + series[-2]
+    for c in series[-3::-1]:
+        total = total * z + c
+    return total
 
 
 def cos_sin(turns):
     r = turns - jnp.round(turns)
-    a = jnp.abs(r)
-    s = quarter_sine(jnp.minimum(a, 0.5 - a))
-    return quarter_sine(0.25 - a), jnp.where(r < 0, -s, s)
+    z = r * r
+    return horner(z, COSINE), horner(z, SINE) * r
 
 
 def frequency_order(width):
@@ -58,7 +55,7 @@
     angle = 2.0 * np.pi * ((b[:, None] * g[None, :]) % width) / width
     dft = np.concatenate([np.cos(angle), np.sin(angle)], axis=1) / width
     tau = g / width + 0.37
-    m = np.arange(1, cols // 2 + 1)
+    m = np.arange(1, 129)
     l = np.arange(8)
     middles = (16 * np.arange(width // 16) + 7.5 - width // 2) / width + 0.37
     side = ((l + 0.5) / width)[:, None] * m[None, :] * 0.05
@@ -147,8 +144,17 @@
     return jnp.concatenate(real + imag, axis=0).astype(jnp.bfloat16)
 
 
-def right_of(p, geo_s, column, at, width):
-    cy, sy = cos_sin(column[:, at : at + 128] * geo_s[2, 0, p])
+def right_of(h, p, geo_s, column, waves, width):
+    if h == 0:
+        cy, sy = cos_sin(column[...] * geo_s[2, 0, p])
+    else:
+        cy, sy = waves[0, p], waves[1, p]
+        ce, se = waves[2, p], waves[3, p]
+        cy, sy = cy * ce - sy * se, sy * ce + cy * se
+    waves[0, p], waves[1, p] = cy, sy
+    if h == 0:
+        waves[2, p] = jnp.broadcast_to(cy[:, 127:128], cy.shape)
+        waves[3, p] = jnp.broadcast_to(sy[:, 127:128], sy.shape)
     c0, s0 = cy[:8], sy[:8]
     right_c, right_s = [], []
     for j in range(width // 16):
@@ -165,33 +171,34 @@
     )
 
 
-def one_pass(h, geo_s, column, row, coef, left_all, acc, slots, width, rows):
+def one_pass(h, geo_s, column, row, coef, left_all, waves, acc, zeros, slots, width, rows):
     acc[...] = jnp.zeros_like(acc)
-
-    def step(i, total):
-        rights = []
+    if h == 0:
+        zeros[...] = jnp.zeros_like(zeros)
+
+    def step(i, _):
+        lefts, rights = [], []
         for k in range(GROUP):
             p = i * GROUP + k
             if h == 0:
-                left = lefts_of(p, geo_s, row, coef, rows)
-                left_all[i, :, k * width : (k + 1) * width] = left
-                total = total + left.astype(jnp.float32)
-            rights.append(right_of(p, geo_s, column, 128 * h, width))
+                lefts.append(lefts_of(p, geo_s, row, coef, rows))
+            rights.append(right_of(h, p, geo_s, column, waves, width))
+        if h == 0:
+            left = jnp.concatenate(lefts, axis=1)
+            left_all[i] = left
+            added = zeros[...]
+            for left_one in lefts:
+                added = added + left_one.astype(jnp.float32)
+            zeros[...] = added
+        else:
+            left = left_all[i]
         acc[...] += jnp.dot(
-            left_all[i],
-            jnp.concatenate(rights, axis=0),
-            preferred_element_type=jnp.float32,
+            left, jnp.concatenate(rights, axis=0), preferred_element_type=jnp.float32
         )
-        return total
-
-    if h == 0:
-        total = lax.fori_loop(
-            0, slots // GROUP, step, jnp.zeros((2 * rows, width), jnp.float32)
-        )
-        zero = jnp.sum(total, axis=1, keepdims=True)
-    else:
-        lax.fori_loop(0, slots // GROUP, step, 0)
-        zero = None
+        return 0
+
+    lax.fori_loop(0, slots // GROUP, step, 0)
+    zero = jnp.sum(zeros[...], axis=1, keepdims=True) if h == 0 else None
     rc, rs = acc[:rows, :128], acc[:rows, 128:]
     ic, is_ = acc[rows:, :128], acc[rows:, 128:]
     ahead = jnp.concatenate([rc - is_, rs + ic], axis=0)
@@ -221,7 +228,9 @@
     cumulative,
     coef,
     left_all,
+    waves,
     acc,
+    zeros,
     mine,
     shares,
     sums,
@@ -274,7 +283,7 @@
     before = None
     for h in range(passes):
         low, ahead, zero = one_pass(
-            h, geo_s, column, row, coef, left_all, acc, slots, width, rows
+            h, geo_s, column, row, coef, left_all, waves, acc, zeros, slots, width, rows
         )
         high = pltpu.roll(ahead, 1, 1)
         edge = lax.broadcasted_iota(jnp.int32, high.shape, 1) == 0
@@ -341,7 +350,9 @@
         scratch_shapes=[
             pltpu.VMEM((2 * (rows // 8), slots, width), jnp.float32),
             pltpu.VMEM((slots // GROUP, 2 * rows, GROUP * width), jnp.bfloat16),
+            pltpu.VMEM((4, slots, 8 + width // 16, 128), jnp.float32),
             pltpu.VMEM((2 * rows, 256), jnp.float32),
+            pltpu.VMEM((2 * rows, width), jnp.float32),
             pltpu.VMEM((passes, members, share, 128), jnp.float32),
             pltpu.VMEM((passes, members, share, 128), jnp.float32),
             pltpu.VMEM((passes, members, 2, share, 128), jnp.float32),

time: 31.4 us -> 28 us (0.89)
  Pallas kernels: 26.5 us -> 23.2 us
    pallas_call x1, Pallas kernels: 25.3 us -> 21.9 us  [shards(): pl.pallas_call(functools.partial(kernel, members, last), out_shape=(whole...]
where the time goes in v4:
time: 28 us; the launch traced here: 27.8 us
  Pallas kernels  23.2 us (83%)
  local copies, waits for them, and re-layouts  3.3 us (12%)
  between operations  1.39 us (5%)
    pallas_call x1, Pallas kernels, shards(): pl.pallas_call(functools.partial(kernel, members, last), out_shape=(whole...  21.9 us
    unnamed x16, local copies, waits for them, and re-layouts  3.3 us
    pallas_call x1, Pallas kernels, shards(): pl.pallas_call(fetch_kernel, out_shape=jax.ShapeDtypeStruct((2 * slots, w...  1.24 us

profile of v4, /device:TPU:0, one launch (start us, length us, event | category | flops | bytes accessed | tf_op | source)
XLA Modules:
  0.0 27.8 jit_solution(18092986178842893004)
XLA Ops:
  0.6 0.0 copy-start.6
  0.6 0.0 copy-start.4
  0.7 0.0 copy-start.3
  1.3 0.0 copy-start
  1.3 1.3 %copy-done = bf16[1,80,2,4096]{3,2,1,0:T(2,128)(2,1)S(1)} copy-done((bf16[1,80,2,4096]{3,2,1,0:T(2,128)(2,1)S(1)}, bf16[1,80,2,4096]{3,2,1,0:T(2,128)(2,1)}, u32[]{:S(2)}) %copy-start) | copy-done | bytes 1310744
  2.7 0.0 copy-start.5
  2.7 0.7 %copy-done.5 = s32[1,80]{1,0:T(1,128)S(1)} copy-done((s32[1,80]{1,0:T(1,128)S(1)}, s32[1,80]{1,0:T(1,128)}, u32[]{:S(2)}) %copy-start.5) | copy-done | bytes 344
  3.3 0.0 copy-start.1
  3.3 0.0 copy-start.2
  3.3 1.2 %shard_map.95.win = f32[160,128]{1,0:T(8,128)S(1)} custom-call(s32[1,80]{1,0:T(1,128)S(1)} %copy-done.5, bf16[1,80,2,4096]{3,2,1,0:T(2,128)(2,1)S(1)} %copy-done), custom_call_target="tpu_custom_call" | custom-call | tf_op jit(solution)/shard_map/pallas_call | solution.py:337
  4.6 0.0 copy-done.6
  4.6 0.0 copy-done.4
  4.6 0.0 copy-done.3
  4.6 0.0 copy-done.1
  4.6 0.0 copy-done.2
  4.6 21.9 %shard_map.96 = (f32[64,512]{1,0:T(8,128)S(1)}, f32[64,512]{1,0:T(8,128)S(1)}) custom-call(f32[3,1,80]{2,1,0:T(1,128)S(1)} %bitcast.5, s32[1]{0:T(128)S(6)} %copy.12.count_s, f32[160,128]{1,0:T(8,128)S(1)} %shard_map.95.win, s32[1,80]{1,0:T(1,128)S(1)} %copy-done.5, f32[3,1,80]{2,1,0:T(1,128)S(1)} %bitcast.6, f32[128,256]{1,0:T(8,128)S(1)} %copy-done.1, ...), custom_call_target="tpu_custom_call" | custom-call | tf_op jit(solution)/shard_map/pallas_call | solution.py:345
  26.5 0.7 %copy.13 = f32[1,2,32,512]{3,2,1,0:T(8,128)} copy(f32[1,2,32,512]{3,2,1,0:T(8,128)S(1)} %bitcast.4) | data formatting | bytes 262144
  27.2 0.7 %copy.14 = f32[1,2,32,512]{3,2,1,0:T(8,128)} copy(f32[1,2,32,512]{3,2,1,0:T(8,128)S(1)} %bitcast.3) | data formatting | bytes 262144
Async XLA Ops:
  0.6 3.9 %copy-start.6 = (f32[2,128]{1,0:T(2,128)S(1)}, f32[2,128]{1,0:T(2,128)}, u32[]{:S(2)}) copy-start(f32[2,128]{1,0:T(2,128)} %constant.11.clone.lead) | copy-start | bytes 3076
  0.6 3.9 %copy-start.4 = (f32[8,128]{1,0:T(8,128)S(1)}, f32[8,128]{1,0:T(8,128)}, u32[]{:S(2)}) copy-start(f32[8,128]{1,0:T(8,128)} %constant.10.clone.row) | copy-start | bytes 12292
  0.7 3.9 %copy-start.3 = (f32[1,3,80]{2,0,1:T(1,128)S(1)}, f32[1,3,80]{2,0,1:T(1,128)}, u32[]{:S(2)}) copy-start(f32[1,3,80]{2,0,1:T(1,128)} %param.10) | copy-start | bytes 2884
  1.3 1.3 %copy-start = (bf16[1,80,2,4096]{3,2,1,0:T(2,128)(2,1)S(1)}, bf16[1,80,2,4096]{3,2,1,0:T(2,128)(2,1)}, u32[]{:S(2)}) copy-start(bf16[1,80,2,4096]{3,2,1,0:T(2,128)(2,1)} %pulses.1) | copy-start | bytes 3932164
  2.7 0.7 %copy-start.5 = (s32[1,80]{1,0:T(1,128)S(1)}, s32[1,80]{1,0:T(1,128)}, u32[]{:S(2)}) copy-start(s32[1,80]{1,0:T(1,128)} %offs_v.1) | copy-start | bytes 964
  3.3 1.3 %copy-start.1 = (f32[128,256]{1,0:T(8,128)S(1)}, f32[128,256]{1,0:T(8,128)}, u32[]{:S(2)}) copy-start(f32[128,256]{1,0:T(8,128)} %constant.8.clone.dft) | copy-start | bytes 393220
  3.3 1.3 %copy-start.2 = (f32[16,128]{1,0:T(8,128)S(1)}, f32[16,128]{1,0:T(8,128)}, u32[]{:S(2)}) copy-start(f32[16,128]{1,0:T(8,128)} %constant.9.clone.column) | copy-start | bytes 24580

commit v5 on v4

--- a/solution.py
+++ b/solution.py
@@ -71,7 +71,7 @@
     )
 
 
-def fetch_kernel(offs_s, pulses, win):
+def fetch_kernel(offs_s, pulses_hbm, win, pulses, arrived):
     slots, width = pulses.shape[1], win.shape[1]
     last = pulses.shape[3] // width - 2
     lanes = lax.broadcasted_iota(jnp.int32, (2, width), 1)
@@ -88,12 +88,24 @@
         win[pl.ds(p, 1), :] = both[0:1]
         win[pl.ds(slots + p, 1), :] = both[1:2]
 
-    def fetch_some(i, _):
-        for k in range(8):
-            fetch(i * 8 + k)
-        return 0
-
-    lax.fori_loop(0, slots // 8, fetch_some, 0)
+    parts = arrived.shape[0]
+    size = slots // parts
+
+    def part(n):
+        at = pl.ds(n * size, size)
+        return pltpu.make_async_copy(pulses_hbm.at[:, at], pulses.at[:, at], arrived.at[n])
+
+    for n in range(parts):
+        part(n).start()
+    for n in range(parts):
+        part(n).wait()
+
+        def fetch_some(i, _, n=n):
+            for k in range(8):
+                fetch(n * size + i * 8 + k)
+            return 0
+
+        lax.fori_loop(0, size // 8, fetch_some, 0)
 
 
 def prepare(count_s, win, offs_v, geo_v, dft, lead, coef, last, rows):
@@ -337,8 +349,12 @@
     win = pl.pallas_call(
         fetch_kernel,
         out_shape=jax.ShapeDtypeStruct((2 * slots, width), jnp.float32),
-        in_specs=[smem, vmem],
+        in_specs=[smem, pl.BlockSpec(memory_space=pltpu.HBM)],
         out_specs=vmem,
+        scratch_shapes=[
+            pltpu.VMEM(pulses.shape, pulses.dtype),
+            pltpu.SemaphoreType.DMA((math.gcd(slots // 8, 5),)),
+        ],
         compiler_params=pltpu.CompilerParams(vmem_limit_bytes=16 * 2**20),
     )(offsets, pulses)
     last = pulses.shape[3] // width - 2

time: 28 us -> 28.2 us (level)
  no operation moved by 1% of the time
where the time goes in v5:
time: 28.2 us; the launch traced here: 28 us
  Pallas kernels  23.3 us (83%)
  local copies, waits for them, and re-layouts  3.3 us (12%)
  between operations  1.39 us (5%)
    pallas_call x1, Pallas kernels, shards(): pl.pallas_call(functools.partial(kernel, members, last), out_shape=(whole...  21.9 us
    unnamed x16, local copies, waits for them, and re-layouts  3.3 us
    pallas_call x1, Pallas kernels, shards(): pl.pallas_call(fetch_kernel, out_shape=jax.ShapeDtypeStruct((2 * slots, w...  1.37 us

profile of v5, /device:TPU:0, one launch (start us, length us, event | category | flops | bytes accessed | tf_op | source)
XLA Modules:
  0.0 28.0 jit_solution(7927616010308094183)
XLA Ops:
  0.6 0.0 copy-start.6
  0.6 0.0 copy-start.4
  0.7 0.0 copy-start.3
  1.3 0.0 copy-start
  1.3 1.3 %copy-done = bf16[1,80,2,4096]{3,2,1,0:T(2,128)(2,1)S(1)} copy-done((bf16[1,80,2,4096]{3,2,1,0:T(2,128)(2,1)S(1)}, bf16[1,80,2,4096]{3,2,1,0:T(2,128)(2,1)}, u32[]{:S(2)}) %copy-start) | copy-done | bytes 1310744
  2.7 0.0 copy-start.5
  2.7 0.7 %copy-done.5 = s32[1,80]{1,0:T(1,128)S(1)} copy-done((s32[1,80]{1,0:T(1,128)S(1)}, s32[1,80]{1,0:T(1,128)}, u32[]{:S(2)}) %copy-start.5) | copy-done | bytes 344
  3.3 0.0 copy-start.1
  3.3 0.0 copy-start.2
  3.3 1.4 %shard_map.95.win = f32[160,128]{1,0:T(8,128)S(1)} custom-call(s32[1,80]{1,0:T(1,128)S(1)} %copy-done.5, bf16[1,80,2,4096]{3,2,1,0:T(2,128)(2,1)S(1)} %copy-done), custom_call_target="tpu_custom_call" | custom-call | tf_op jit(solution)/shard_map/pallas_call | solution.py:349
  4.7 0.0 copy-done.6
  4.7 0.0 copy-done.4
  4.7 0.0 copy-done.3
  4.7 0.0 copy-done.1
  4.7 0.0 copy-done.2
  4.7 21.9 %shard_map.96 = (f32[64,512]{1,0:T(8,128)S(1)}, f32[64,512]{1,0:T(8,128)S(1)}) custom-call(f32[3,1,80]{2,1,0:T(1,128)S(1)} %bitcast.5, s32[1]{0:T(128)S(6)} %copy.12.count_s, f32[160,128]{1,0:T(8,128)S(1)} %shard_map.95.win, s32[1,80]{1,0:T(1,128)S(1)} %copy-done.5, f32[3,1,80]{2,1,0:T(1,128)S(1)} %bitcast.6, f32[128,256]{1,0:T(8,128)S(1)} %copy-done.1, ...), custom_call_target="tpu_custom_call" | custom-call | tf_op jit(solution)/shard_map/pallas_call | solution.py:361
  26.7 0.7 %copy.13 = f32[1,2,32,512]{3,2,1,0:T(8,128)} copy(f32[1,2,32,512]{3,2,1,0:T(8,128)S(1)} %bitcast.4) | data formatting | bytes 262144
  27.3 0.7 %copy.14 = f32[1,2,32,512]{3,2,1,0:T(8,128)} copy(f32[1,2,32,512]{3,2,1,0:T(8,128)S(1)} %bitcast.3) | data formatting | bytes 262144
Async XLA Ops:
  0.6 4.1 %copy-start.6 = (f32[2,128]{1,0:T(2,128)S(1)}, f32[2,128]{1,0:T(2,128)}, u32[]{:S(2)}) copy-start(f32[2,128]{1,0:T(2,128)} %constant.11.clone.lead) | copy-start | bytes 3076
  0.6 4.1 %copy-start.4 = (f32[8,128]{1,0:T(8,128)S(1)}, f32[8,128]{1,0:T(8,128)}, u32[]{:S(2)}) copy-start(f32[8,128]{1,0:T(8,128)} %constant.10.clone.row) | copy-start | bytes 12292
  0.7 4.1 %copy-start.3 = (f32[1,3,80]{2,0,1:T(1,128)S(1)}, f32[1,3,80]{2,0,1:T(1,128)}, u32[]{:S(2)}) copy-start(f32[1,3,80]{2,0,1:T(1,128)} %param.10) | copy-start | bytes 2884
  1.3 1.3 %copy-start = (bf16[1,80,2,4096]{3,2,1,0:T(2,128)(2,1)S(1)}, bf16[1,80,2,4096]{3,2,1,0:T(2,128)(2,1)}, u32[]{:S(2)}) copy-start(bf16[1,80,2,4096]{3,2,1,0:T(2,128)(2,1)} %pulses_hbm.1) | copy-start | bytes 3932164
  2.7 0.7 %copy-start.5 = (s32[1,80]{1,0:T(1,128)S(1)}, s32[1,80]{1,0:T(1,128)}, u32[]{:S(2)}) copy-start(s32[1,80]{1,0:T(1,128)} %offs_v.1) | copy-start | bytes 964
  3.3 1.4 %copy-start.1 = (f32[128,256]{1,0:T(8,128)S(1)}, f32[128,256]{1,0:T(8,128)}, u32[]{:S(2)}) copy-start(f32[128,256]{1,0:T(8,128)} %constant.8.clone.dft) | copy-start | bytes 393220
  3.3 1.4 %copy-start.2 = (f32[16,128]{1,0:T(8,128)S(1)}, f32[16,128]{1,0:T(8,128)}, u32[]{:S(2)}) copy-start(f32[16,128]{1,0:T(8,128)} %constant.9.clone.column) | copy-start | bytes 24580

commit v6 on v5

--- a/solution.py
+++ b/solution.py
@@ -355,7 +355,6 @@
             pltpu.VMEM(pulses.shape, pulses.dtype),
             pltpu.SemaphoreType.DMA((math.gcd(slots // 8, 5),)),
         ],
-        compiler_params=pltpu.CompilerParams(vmem_limit_bytes=16 * 2**20),
     )(offsets, pulses)
     last = pulses.shape[3] // width - 2
     frames, cumulative = pl.pallas_call(

time: 28.2 us -> 28.7 us (1.018)
  Pallas kernels: 23.3 us -> 24.9 us
  local copies, waits for them, and re-layouts: 3.3 us -> 2.23 us
    pallas_call x1, Pallas kernels: 1.37 us -> 2.97 us  [shards(): pl.pallas_call(fetch_kernel, out_shape=jax.ShapeDtypeStruct((2 * slots, w...]
    unnamed x16, local copies, waits for them, and re-layouts: 3.3 us -> 2.23 us
where the time goes in v6:
time: 28.7 us; the launch traced here: 28.5 us
  Pallas kernels  24.9 us (87%)
  local copies, waits for them, and re-layouts  2.23 us (8%)
  between operations  1.44 us (5%)
    pallas_call x1, Pallas kernels, shards(): pl.pallas_call(functools.partial(kernel, members, last), out_shape=(whole...  21.9 us
    pallas_call x1, Pallas kernels, shards(): pl.pallas_call(fetch_kernel, out_shape=jax.ShapeDtypeStruct((2 * slots, w...  2.97 us
    unnamed x16, local copies, waits for them, and re-layouts  2.23 us

profile of v6, /device:TPU:0, one launch (start us, length us, event | category | flops | bytes accessed | tf_op | source)
XLA Modules:
  0.0 28.5 jit_solution(17479303103485030326)
XLA Ops:
  0.6 0.0 copy-start.6
  0.6 0.0 copy-start.4
  0.7 0.0 copy-start.2
  0.7 0.0 copy-start.1
  0.7 0.0 copy-start.5
  0.7 0.0 copy-start.3
  1.4 3.0 %shard_map.95.win = f32[160,128]{1,0:T(8,128)} custom-call(s32[1,80]{1,0:T(1,128)} %offs_v.1, bf16[1,80,2,4096]{3,2,1,0:T(2,128)(2,1)} %pulses_hbm.1), custom_call_target="tpu_custom_call" | custom-call | tf_op jit(solution)/shard_map/pallas_call | solution.py:349
  4.4 0.0 copy-done.6
  4.4 0.0 copy-done.4
  4.4 0.0 copy-done.2
  4.4 0.0 copy-done.1
  4.4 0.0 copy-done.5
  4.4 0.0 copy-done.3
  4.4 0.0 copy-start
  4.4 0.9 %copy-done = f32[160,128]{1,0:T(8,128)S(1)} copy-done((f32[160,128]{1,0:T(8,128)S(1)}, f32[160,128]{1,0:T(8,128)}, u32[]{:S(2)}) %copy-start) | copy-done | bytes 81944
  5.3 21.9 %shard_map.96 = (f32[64,512]{1,0:T(8,128)S(1)}, f32[64,512]{1,0:T(8,128)S(1)}) custom-call(f32[3,1,80]{2,1,0:T(1,128)S(1)} %bitcast.5, s32[1]{0:T(128)S(6)} %copy.12.count_s, f32[160,128]{1,0:T(8,128)S(1)} %copy-done, s32[1,80]{1,0:T(1,128)S(1)} %copy-done.5, f32[3,1,80]{2,1,0:T(1,128)S(1)} %bitcast.6, f32[128,256]{1,0:T(8,128)S(1)} %copy-done.1, ...), custom_call_target="tpu_custom_call" | custom-call | tf_op jit(solution)/shard_map/pallas_call | solution.py:360
  27.2 0.7 %copy.13 = f32[1,2,32,512]{3,2,1,0:T(8,128)} copy(f32[1,2,32,512]{3,2,1,0:T(8,128)S(1)} %bitcast.4) | data formatting | bytes 262144
  27.9 0.7 %copy.14 = f32[1,2,32,512]{3,2,1,0:T(8,128)} copy(f32[1,2,32,512]{3,2,1,0:T(8,128)S(1)} %bitcast.3) | data formatting | bytes 262144
Async XLA Ops:
  0.6 3.7 %copy-start.6 = (f32[2,128]{1,0:T(2,128)S(1)}, f32[2,128]{1,0:T(2,128)}, u32[]{:S(2)}) copy-start(f32[2,128]{1,0:T(2,128)} %constant.11.clone.lead) | copy-start | bytes 3076
  0.6 3.7 %copy-start.4 = (f32[8,128]{1,0:T(8,128)S(1)}, f32[8,128]{1,0:T(8,128)}, u32[]{:S(2)}) copy-start(f32[8,128]{1,0:T(8,128)} %constant.10.clone.row) | copy-start | bytes 12292
  0.7 3.7 %copy-start.2 = (f32[16,128]{1,0:T(8,128)S(1)}, f32[16,128]{1,0:T(8,128)}, u32[]{:S(2)}) copy-start(f32[16,128]{1,0:T(8,128)} %constant.9.clone.column) | copy-start | bytes 24580
  0.7 3.7 %copy-start.1 = (f32[128,256]{1,0:T(8,128)S(1)}, f32[128,256]{1,0:T(8,128)}, u32[]{:S(2)}) copy-start(f32[128,256]{1,0:T(8,128)} %constant.8.clone.dft) | copy-start | bytes 393220
  0.7 3.7 %copy-start.5 = (s32[1,80]{1,0:T(1,128)S(1)}, s32[1,80]{1,0:T(1,128)}, u32[]{:S(2)}) copy-start(s32[1,80]{1,0:T(1,128)} %offs_v.1) | copy-start | bytes 964
  0.7 3.7 %copy-start.3 = (f32[1,3,80]{2,0,1:T(1,128)S(1)}, f32[1,3,80]{2,0,1:T(1,128)}, u32[]{:S(2)}) copy-start(f32[1,3,80]{2,0,1:T(1,128)} %param.10) | copy-start | bytes 2884
  4.4 0.9 %copy-start = (f32[160,128]{1,0:T(8,128)S(1)}, f32[160,128]{1,0:T(8,128)}, u32[]{:S(2)}) copy-start(f32[160,128]{1,0:T(8,128)} %shard_map.95.win) | copy-start | bytes 245764

commit v7 on v4

--- a/solution.py
+++ b/solution.py
@@ -12,7 +12,7 @@
 ROWS = 32
 COLS = 512
 BINS = 128
-GROUP = 8
+GROUP = 16
 HIGHEST = lax.Precision.HIGHEST
 
 def _series(count, odd):

time: 28 us -> 27 us (0.964)
  Pallas kernels: 23.2 us -> 22.1 us
    pallas_call x1, Pallas kernels: 21.9 us -> 20.9 us  [shards(): pl.pallas_call(functools.partial(kernel, members, last), out_shape=(whole...]
where the time goes in v7:
time: 27 us; the launch traced here: 26.8 us
  Pallas kernels  22.1 us (82%)
  local copies, waits for them, and re-layouts  3.3 us (12%)
  between operations  1.39 us (5%)
    pallas_call x1, Pallas kernels, shards(): pl.pallas_call(functools.partial(kernel, members, last), out_shape=(whole...  20.9 us
    unnamed x16, local copies, waits for them, and re-layouts  3.3 us
    pallas_call x1, Pallas kernels, shards(): pl.pallas_call(fetch_kernel, out_shape=jax.ShapeDtypeStruct((2 * slots, w...  1.24 us

profile of v7, /device:TPU:0, one launch (start us, length us, event | category | flops | bytes accessed | tf_op | source)
XLA Modules:
  0.0 26.8 jit_solution(4137923300155192622)
XLA Ops:
  0.6 0.0 copy-start.6
  0.6 0.0 copy-start.4
  0.7 0.0 copy-start.3
  1.3 0.0 copy-start
  1.3 1.3 %copy-done = bf16[1,80,2,4096]{3,2,1,0:T(2,128)(2,1)S(1)} copy-done((bf16[1,80,2,4096]{3,2,1,0:T(2,128)(2,1)S(1)}, bf16[1,80,2,4096]{3,2,1,0:T(2,128)(2,1)}, u32[]{:S(2)}) %copy-start) | copy-done | bytes 1310744
  2.7 0.0 copy-start.5
  2.7 0.7 %copy-done.5 = s32[1,80]{1,0:T(1,128)S(1)} copy-done((s32[1,80]{1,0:T(1,128)S(1)}, s32[1,80]{1,0:T(1,128)}, u32[]{:S(2)}) %copy-start.5) | copy-done | bytes 344
  3.3 0.0 copy-start.1
  3.3 0.0 copy-start.2
  3.3 1.2 %shard_map.95.win = f32[160,128]{1,0:T(8,128)S(1)} custom-call(s32[1,80]{1,0:T(1,128)S(1)} %copy-done.5, bf16[1,80,2,4096]{3,2,1,0:T(2,128)(2,1)S(1)} %copy-done), custom_call_target="tpu_custom_call" | custom-call | tf_op jit(solution)/shard_map/pallas_call | solution.py:337
  4.6 0.0 copy-done.6
  4.6 0.0 copy-done.4
  4.6 0.0 copy-done.3
  4.6 0.0 copy-done.1
  4.6 0.0 copy-done.2
  4.6 20.9 %shard_map.96 = (f32[64,512]{1,0:T(8,128)S(1)}, f32[64,512]{1,0:T(8,128)S(1)}) custom-call(f32[3,1,80]{2,1,0:T(1,128)S(1)} %bitcast.5, s32[1]{0:T(128)S(6)} %copy.12.count_s, f32[160,128]{1,0:T(8,128)S(1)} %shard_map.95.win, s32[1,80]{1,0:T(1,128)S(1)} %copy-done.5, f32[3,1,80]{2,1,0:T(1,128)S(1)} %bitcast.6, f32[128,256]{1,0:T(8,128)S(1)} %copy-done.1, ...), custom_call_target="tpu_custom_call" | custom-call | tf_op jit(solution)/shard_map/pallas_call | solution.py:345
  25.5 0.7 %copy.13 = f32[1,2,32,512]{3,2,1,0:T(8,128)} copy(f32[1,2,32,512]{3,2,1,0:T(8,128)S(1)} %bitcast.4) | data formatting | bytes 262144
  26.2 0.7 %copy.14 = f32[1,2,32,512]{3,2,1,0:T(8,128)} copy(f32[1,2,32,512]{3,2,1,0:T(8,128)S(1)} %bitcast.3) | data formatting | bytes 262144
Async XLA Ops:
  0.6 3.9 %copy-start.6 = (f32[2,128]{1,0:T(2,128)S(1)}, f32[2,128]{1,0:T(2,128)}, u32[]{:S(2)}) copy-start(f32[2,128]{1,0:T(2,128)} %constant.11.clone.lead) | copy-start | bytes 3076
  0.6 3.9 %copy-start.4 = (f32[8,128]{1,0:T(8,128)S(1)}, f32[8,128]{1,0:T(8,128)}, u32[]{:S(2)}) copy-start(f32[8,128]{1,0:T(8,128)} %constant.10.clone.row) | copy-start | bytes 12292
  0.7 3.9 %copy-start.3 = (f32[1,3,80]{2,0,1:T(1,128)S(1)}, f32[1,3,80]{2,0,1:T(1,128)}, u32[]{:S(2)}) copy-start(f32[1,3,80]{2,0,1:T(1,128)} %param.10) | copy-start | bytes 2884
  1.3 1.3 %copy-start = (bf16[1,80,2,4096]{3,2,1,0:T(2,128)(2,1)S(1)}, bf16[1,80,2,4096]{3,2,1,0:T(2,128)(2,1)}, u32[]{:S(2)}) copy-start(bf16[1,80,2,4096]{3,2,1,0:T(2,128)(2,1)} %pulses.1) | copy-start | bytes 3932164
  2.7 0.7 %copy-start.5 = (s32[1,80]{1,0:T(1,128)S(1)}, s32[1,80]{1,0:T(1,128)}, u32[]{:S(2)}) copy-start(s32[1,80]{1,0:T(1,128)} %offs_v.1) | copy-start | bytes 964
  3.3 1.3 %copy-start.1 = (f32[128,256]{1,0:T(8,128)S(1)}, f32[128,256]{1,0:T(8,128)}, u32[]{:S(2)}) copy-start(f32[128,256]{1,0:T(8,128)} %constant.8.clone.dft) | copy-start | bytes 393220
  3.3 1.3 %copy-start.2 = (f32[16,128]{1,0:T(8,128)S(1)}, f32[16,128]{1,0:T(8,128)}, u32[]{:S(2)}) copy-start(f32[16,128]{1,0:T(8,128)} %constant.9.clone.column) | copy-start | bytes 24580
